TPU v7x, 32 devices: a whole 2x2x4 slice. The times are simulated.
32 devices in a mesh: batch: 8 (over z, x), head: 4 (over y, core).
Axes of the slice: x: 2, y: 2, z: 4, core: 2. Of those that a mesh axis runs over, the one named last changes fastest.
Arguments:
- tokens: bfloat16 [8, 2048, 768], P('batch', 'head'), may hold values from -6 to 6
- lengths: int32 [8], P('batch'), may hold values from 1024 to 2048, as said below
- w_query: bfloat16 [768, 768], P(None, 'head'), may hold values from -0.3125 to 0.3125
- w_key: bfloat16 [768, 768], P(None, 'head'), may hold values from -0.3125 to 0.3125
- w_value: bfloat16 [768, 768], P(None, 'head'), may hold values from -0.21875 to 0.21875
- w_out: bfloat16 [768, 768], P('head'), may hold values from -0.4375 to 0.4375
- conv_taps: float32 [12, 65], P('head'), may hold values from -0.875 to 0.875
- w_up: bfloat16 [768, 3072], P(None, 'head'), may hold values from -0.21875 to 0.21875
- b_up: float32 [3072], P('head'), may hold values from -3 to 3
- w_down: bfloat16 [3072, 768], P('head'), may hold values from -0.109375 to 0.109375
- gain_attn: float32 [768], replicated, may hold values from 0.5 to 1.5
- shift_attn: float32 [768], replicated, may hold values from -1.75 to 1.75
- gain_ffn: float32 [768], replicated, may hold values from 0.5 to 1.5
- shift_ffn: float32 [768], replicated, may hold values from -1.75 to 1.75
- grad_out: bfloat16 [8, 2048, 768], P('batch', 'head'), may hold values from -6 to 6
Outputs:
- output: bfloat16 [8, 2048, 768], P('batch', 'head')
- d_tokens: float32 [8, 2048, 768], P('batch', 'head')
- d_w_query: float32 [768, 768], P(None, 'head')
- d_w_key: float32 [768, 768], P(None, 'head')
- d_w_value: float32 [768, 768], P(None, 'head')
- d_w_out: float32 [768, 768], P('head')
- d_conv_taps: float32 [12, 65], P('head')
- d_w_up: float32 [768, 3072], P(None, 'head')
- d_b_up: float32 [3072], P('head')
- d_w_down: float32 [3072, 768], P('head')
- d_gain_attn: float32 [768], replicated
- d_shift_attn: float32 [768], replicated
- d_gain_ffn: float32 [768], replicated
- d_shift_ffn: float32 [768], replicated
Inputs may be any that keep to these rules, and one draw needn't show every extreme that they name: `lengths`: the true length of each sequence; in every draw one sequence is exactly 2048 long.
All inputs are finite; a program needn't handle non-finite values.
Results may differ from a plain program's by a relative error of at most 0.015.
Values may be sent and summed in bfloat16 or wider, within the bound.
No kernel may reach another device: no remote copies, remote signals or barrier semaphores. Data moves between devices by JAX's collectives and lax.ppermute only.
A program may use at most 320 MiB of HBM per device.

v0:
```python
import functools

import jax
import jax.numpy as jnp
from jax import lax
from jax.experimental import pallas as pl
from jax.experimental.pallas import tpu as pltpu
from jax.sharding import PartitionSpec as P

f32 = jnp.float32
bf16 = jnp.bfloat16
HEAD_DIM = 64
LANDMARKS = 64
NEWTON = 6
TAPS = 65
HALO = TAPS // 2
EARLY = 1
LATE = 0
IDLE = 1
GROUP = 256
NN = ((1,), (0,))
NT = ((1,), (1,))
TN = ((0,), (0,))
VMEM = pltpu.VMEM
ANY = pl.ANY


def dot(a, b, dims=NN):
    return lax.dot_general(a, b, (dims, ((), ())), preferred_element_type=f32)


def split(x):
    high = x.astype(bf16)
    return high, (x - high.astype(f32)).astype(bf16)


def mm(a, b, dims=NN):
    a_high, a_low = split(a)
    b_high, b_low = split(b)
    return dot(a_high, b_high, dims) + (dot(a_high, b_low, dims) + dot(a_low, b_high, dims))


def mm_left(a, b, dims=NN):
    a_high, a_low = split(a)
    return dot(a_high, b, dims) + dot(a_low, b, dims)


def iota(shape, dim):
    return lax.broadcasted_iota(jnp.int32, shape, dim)


def call(body, outs, ins, scratch=(), flops=0, size=0, limit=40, name=None, smem=()):
    specs = [
        pl.BlockSpec(memory_space=pltpu.SMEM) if i in smem else pl.BlockSpec(memory_space=space)
        for i, (space, _) in enumerate(ins)
    ]
    return pl.pallas_call(
        body,
        out_shape=[jax.ShapeDtypeStruct(s, d) for s, d in outs],
        in_specs=specs,
        out_specs=[pl.BlockSpec(memory_space=VMEM)] * len(outs),
        scratch_shapes=list(scratch),
        compiler_params=pltpu.CompilerParams(vmem_limit_bytes=limit << 20),
        cost_estimate=pl.CostEstimate(flops=flops, bytes_accessed=size, transcendentals=0),
        name=name,
    )(*[value for _, value in ins])


def call_many(parts, name):
    ins = [value for part in parts for value in part[2]]
    outs = [value for part in parts for value in part[1]]
    scratch = [value for part in parts for value in part[3]]
    smem, first = [], 0
    for part in parts:
        smem += [first + i for i in part[4]]
        first += len(part[2])

    def body(*refs):
        groups = [refs[: len(ins)], refs[len(ins) : len(ins) + len(outs)], refs[len(ins) + len(outs) :]]
        at = [0, 0, 0]
        for part in parts:
            mine = []
            for group, kind in ((0, 2), (1, 1), (2, 3)):
                mine += groups[group][at[group] : at[group] + len(part[kind])]
                at[group] += len(part[kind])
            part[0](*mine)

    results = call(body, outs, ins, scratch, flops=int(5e9), size=10 << 20, name=name, smem=tuple(smem), limit=48)
    split_results, first = [], 0
    for part in parts:
        split_results.append(results[first : first + len(part[1])])
        first += len(part[1])
    return split_results


def block_mask():
    return (iota((GROUP, GROUP), 0) >> 6) == (iota((GROUP, GROUP), 1) >> 6)


def spread(x):
    return jnp.where(block_mask(), jnp.concatenate([x, x, x, x], axis=0), 0.0)


def fold(x):
    kept = jnp.where(block_mask(), x, 0.0)
    return kept[0:64] + kept[64:128] + kept[128:192]


def rows_of(info, count, first):
    return info[1] + first + iota((count, 1), 0)


def landmark_kernel(p0, p1, p2, p3, wt, lm, pool, chain):
    pooled = (p0[...].astype(f32) + p1[...].astype(f32)) + (p2[...].astype(f32) + p3[...].astype(f32))
    pool[...] = pooled.astype(bf16)
    high, low = split(pooled)
    both = jnp.concatenate([high, low], axis=0)
    lm[...] = jnp.zeros_like(lm)
    matrices, starts = [], []
    for head in range(3):
        pair = []
        for kind in range(2):
            rows = wt[kind * 192 + head * 64 : kind * 192 + head * 64 + 64]
            out = dot(both, rows, NT)
            out = out[0:64] + out[64:128]
            lm[:, kind * GROUP + head * 64 : kind * GROUP + head * 64 + 64] = out
            pair.append(out)
        scores = mm(pair[0], pair[1], NT) * 0.125
        raised = jnp.exp(scores - jnp.max(scores, axis=1, keepdims=True))
        matrix = raised / jnp.sum(raised, axis=1, keepdims=True)
        column = jnp.max(jnp.sum(matrix, axis=0, keepdims=True), axis=1, keepdims=True)
        row = jnp.max(jnp.sum(matrix, axis=1, keepdims=True), axis=0, keepdims=True)
        matrices.append(matrix)
        starts.append(matrix.T / (column * row))
    eye = (iota((64, 64), 0) == iota((64, 64), 1)).astype(f32)

    def step(it, iterates):
        results = []
        for head in range(3):
            z = iterates[head]
            product = mm(matrices[head], z)
            inner1 = 7.0 * eye - product
            inner2 = 15.0 * eye - mm(product, inner1)
            inner3 = 13.0 * eye - mm(product, inner2)
            chain[it, 0, head] = z
            chain[it, 1, head] = product
            chain[it, 2, head] = inner2
            chain[it, 3, head] = inner3
            results.append(0.25 * mm(z, inner3))
        return tuple(results)

    finals = lax.fori_loop(0, NEWTON, step, tuple(starts))
    for head in range(3):
        lm[:, 2 * GROUP + head * 64 : 2 * GROUP + head * 64 + 64] = finals[head]


def inverse_back_kernel(x0, x1, wst_all, lm, chain, partial, out):
    total = x0[0] + x1[1]
    eye = (iota((64, 64), 0) == iota((64, 64), 1)).astype(f32)
    weight = wst_all[0]
    out[...] = partial[...].astype(bf16)
    grads, matrices, queries, keys = [], [], [], []
    for head in range(3):
        at = slice(head * 64, head * 64 + 64)
        grads.append(mm(total[:, at], weight[:, at], NT))
        query = lm[:, head * 64 : head * 64 + 64]
        key = lm[:, GROUP + head * 64 : GROUP + head * 64 + 64]
        scores = mm(query, key, NT) * 0.125
        raised = jnp.exp(scores - jnp.max(scores, axis=1, keepdims=True))
        matrices.append(raised / jnp.sum(raised, axis=1, keepdims=True))
        queries.append(query)
        keys.append(key)

    def step(count, carried):
        it = NEWTON - 1 - count
        results = []
        for head in range(3):
            dz_next, da = carried[2 * head], carried[2 * head + 1]
            z = chain[it, 0, head]
            product = chain[it, 1, head]
            inner1 = 7.0 * eye - product
            inner2 = chain[it, 2, head]
            inner3 = chain[it, 3, head]
            dz_next = 0.25 * dz_next
            dz = mm(dz_next, inner3, NT)
            d3 = -mm(z, dz_next, TN)
            d2 = -mm(product, d3, TN)
            d1 = mm(product, d2, TN)
            dp = mm(d3, inner2, NT) + mm(d2, inner1, NT) - d1
            da = da + mm(dp, z, NT)
            dz = dz + mm(matrices[head], dp, TN)
            results += [dz, da]
        return tuple(results)

    first = []
    for head in range(3):
        first += [grads[head], jnp.zeros((64, 64), f32)]
    last = lax.fori_loop(0, NEWTON, step, tuple(first))
    for head in range(3):
        dz, da = last[2 * head], last[2 * head + 1]
        matrix = matrices[head]
        columns = jnp.sum(matrix, axis=0, keepdims=True)
        rows = jnp.sum(matrix, axis=1, keepdims=True)
        column = jnp.max(columns, axis=1, keepdims=True)
        row = jnp.max(rows, axis=0, keepdims=True)
        scale = 1.0 / (column * row)
        da = da + dz.T * scale
        d_scale = -jnp.sum(jnp.sum(dz * matrix.T, axis=1, keepdims=True), axis=0, keepdims=True) * scale * scale
        column_hit = (columns == column).astype(f32)
        row_hit = (rows == row).astype(f32)
        da = da + d_scale * row * column_hit / jnp.sum(column_hit, axis=1, keepdims=True)
        da = da + d_scale * column * row_hit / jnp.sum(row_hit, axis=0, keepdims=True)
        ds = matrix * (da - jnp.sum(da * matrix, axis=1, keepdims=True)) * 0.125
        for at, value in ((head * 64, mm(ds, keys[head])), (GROUP + head * 64, mm(ds, queries[head], TN))):
            out[0, :, at : at + 64] = (partial[0, :, at : at + 64] + value).astype(bf16)


PROJECTION = ((0, 192, 0), (192, 192, GROUP), (384, 192, 2 * GROUP))


def split_copies(refs, parts, held, sems, side):
    own, across, across_x, other, both, both_x = refs
    half = own.shape[1] // 2
    mine = pl.ds(pl.multiple_of(side * half, half), half)
    rest = pl.ds(pl.multiple_of((1 - side) * half, half), half)
    blocks = [[], [], [], []]
    for n, (row, rows, to) in enumerate(parts):
        first = pl.ds(row - parts[0][0], rows)
        source, to = pl.ds(row, rows), pl.ds(to, rows)
        blocks[0].append(pltpu.make_async_copy(own.at[first], held.at[0, to], sems.at[0, n, 0]))
        blocks[2].append(pltpu.make_async_copy(other.at[source], held.at[2, to], sems.at[2, n, 0]))
        for i, near, far in ((1, across, across_x), (3, both, both_x)):
            blocks[i].append(pltpu.make_async_copy(near.at[source], held.at[i, to, mine], sems.at[i, n, 0]))
            blocks[i].append(pltpu.make_async_copy(far.at[source], held.at[i, to, rest], sems.at[i, n, 1]))
    return blocks


def start(copies):
    for block in copies:
        for copy in block:
            copy.start()


def wait(copies, i):
    for block in range(4):

        @pl.when(i == block)
        def _():
            for copy in copies[block]:
                copy.wait()


def zero_gaps(held, kinds):
    for i in range(4):
        for kind in range(kinds):
            held[i, kind * GROUP + 192 : kind * GROUP + 256, :] = jnp.zeros((64, held.shape[2]), bf16)


def project_kernel(info, tokens, before, after, w0, w1, w2, w3, w4, w5, q_out, k_out, v_out, held, sems):
    count = tokens.shape[0]
    copies = split_copies((w0, w1, w2, w3, w4, w5), PROJECTION, held, sems, info[2])
    start(copies)
    zero_gaps(held, 3)
    valid = (rows_of(info, count, 0) < info[0]).astype(f32)
    valid_before = (rows_of(info, HALO, -HALO) < info[0]).astype(f32)
    valid_after = (rows_of(info, HALO, count) < info[0]).astype(f32)

    def body(i, _):
        wait(copies, i)
        for kind, out in ((0, q_out), (1, k_out)):
            out[i] = (dot(tokens[...], held[i, kind * GROUP : kind * GROUP + GROUP], NT) * valid).astype(bf16)
        wv = held[i, 2 * GROUP : 3 * GROUP]
        v_out[i, HALO : HALO + count] = (dot(tokens[...], wv, NT) * valid).astype(bf16)
        v_out[i, 0:HALO] = (dot(before[...], wv, NT) * valid_before).astype(bf16)
        v_out[i, HALO + count : 2 * HALO + count] = (dot(after[...], wv, NT) * valid_after).astype(bf16)
        v_out[i, 2 * HALO + count :] = jnp.zeros((v_out.shape[1] - 2 * HALO - count, GROUP), bf16)
        return 0

    lax.fori_loop(0, 4, body, 0)


def third_scores(info, lm, k_ref, i):
    count = k_ref.shape[1]
    valid = info[1] + iota((1, count), 1) < info[0]
    queries = spread(lm[i, :, 0:GROUP])
    return jnp.where(valid, mm_left(queries, k_ref[i], NT) * 0.125, -1e30)


def third_kernel(info, lm, k_ref, v_ref, pay):
    count = k_ref.shape[1]
    lane = iota((64, GROUP), 1)

    def body(i, _):
        scores = third_scores(info, lm, k_ref, i)
        top = jnp.max(scores, axis=1, keepdims=True)
        raised = jnp.exp(scores - top)
        total = jnp.sum(raised, axis=1, keepdims=True)
        packed = fold(mm_left(raised, v_ref[i, HALO : HALO + count]) / total)
        for stat, base in ((top, 192), (total, 216)):
            for term in range(3):
                part = stat.astype(bf16).astype(f32)
                stat = stat - part
                for head in range(3):
                    packed = jnp.where(lane == base + 8 * term + head, part[head * 64 : head * 64 + 64], packed)
        pay[i] = packed.astype(bf16)
        return 0

    lax.fori_loop(0, 4, body, 0)


def first_scores(lm, q_ref, i):
    keys = spread(lm[i, :, GROUP : 2 * GROUP])
    count = q_ref.shape[1]
    scores = (mm_left(keys, q_ref[i], NT) * 0.125).reshape(4, 64, count)
    raised = jnp.exp(scores - jnp.max(scores, axis=1, keepdims=True))
    return raised / jnp.sum(raised, axis=1, keepdims=True)


def toeplitz(row):
    return pltpu.roll(jnp.broadcast_to(row, (128, GROUP)), 0, 1, stride=1, stride_axis=0)


def head_select(x, rows):
    lane = iota((rows, GROUP), 1) >> 6
    out = jnp.where(lane == 0, x[0:rows], 0.0)
    out = jnp.where(lane == 1, x[rows : 2 * rows], out)
    return jnp.where(lane == 2, x[2 * rows : 3 * rows], out)


def context_kernel(p0, p1, p2, p3, lm, q_ref, v_ref, small, ctx, wst, x_out):
    count = q_ref.shape[1]
    lane = iota((64, GROUP), 1)

    def body(i, _):
        parts = [p[i ^ n].astype(f32) for n, p in enumerate((p0, p1, p2, p3))]

        def stat(part, at):
            return part[:, at : at + 1] + part[:, at + 8 : at + 9] + part[:, at + 16 : at + 17]

        factors = [jnp.zeros((64, GROUP), f32) for _ in range(4)]
        stats = jnp.zeros((64, GROUP), f32)
        for head in range(3):
            tops = [stat(part, 192 + head) for part in parts]
            top = jnp.maximum(jnp.maximum(tops[0], tops[1]), jnp.maximum(tops[2], tops[3]))
            scales = [stat(part, 216 + head) * jnp.exp(t - top) for part, t in zip(parts, tops)]
            total = sum(scales)
            mine = (lane >> 6) == head
            factors = [jnp.where(mine, s / total, f) for s, f in zip(scales, factors)]
            stats = jnp.where(lane == 192 + head, top, stats)
            stats = jnp.where(lane == 196 + head, total, stats)
        weight = sum(part * f for part, f in zip(parts, factors))
        wst[i] = jnp.where(lane < 192, weight, stats)
        mixed = mm(spread(lm[i, :, 2 * GROUP : 3 * GROUP]), spread(weight))
        x_out[i] = fold(mixed)
        first = first_scores(lm, q_ref, i).reshape(GROUP, count)
        main = mm(first, mixed, TN)
        bands = [toeplitz(small[i, 1 + head : 2 + head, 0:GROUP]) for head in range(3)]
        high, low = split(jnp.concatenate(bands, axis=0))
        for block in range(count // 128):
            window = v_ref[i, block * 128 : block * 128 + 256]
            conv = dot(high, window) + dot(low, window)
            ctx[i, block * 128 : block * 128 + 128] = (
                main[block * 128 : block * 128 + 128] + head_select(conv, 128)
            ).astype(bf16)
        return 0

    lax.fori_loop(0, 4, body, 0)


def first_back_kernel(
    info, g_ref, before, after, o0, o1, o2, o3, o4, o5, lm, q_ref, v_ref, small, x_in, dx, dq, dkl, dv, dtaps, held, sems, ext, dctx
):
    count = g_ref.shape[0]
    width = g_ref.shape[1]
    copies = split_copies((o0, o1, o2, o3, o4, o5), ((0, 192, 0),), held, sems, info[2])
    start(copies)
    zero_gaps(held, 1)
    valid = (rows_of(info, count, 0) < info[0]).astype(f32)
    ext[0:HALO] = before[...]
    ext[HALO : HALO + count] = g_ref[...]
    ext[HALO + count : 2 * HALO + count] = after[...]
    ext[2 * HALO + count :] = jnp.zeros((ext.shape[0] - 2 * HALO - count, width), bf16)
    lane = iota((128, GROUP), 1) >> 6
    flip = (iota((128, 128), 0) + iota((128, 128), 1) == 127).astype(bf16)

    def body(i, _):
        wait(copies, i)
        dctx[...] = dot(ext[...], held[i], NT)
        own = dctx[HALO : HALO + count]
        own_high = own.astype(bf16)
        first = first_scores(lm, q_ref, i)
        flat = first.reshape(GROUP, count)
        dx[i] = fold(dot(flat.astype(bf16), own_high))
        dfirst = dot(spread(x_in[i]).astype(bf16), own_high, NT)
        dfirst = dfirst.reshape(4, 64, count)
        ds = first * (dfirst - jnp.sum(first * dfirst, axis=1, keepdims=True)) * 0.125
        ds = ds.reshape(GROUP, count).astype(bf16)
        keys = (spread(lm[i, :, GROUP : 2 * GROUP])).astype(bf16)
        dquery = dot(ds, keys, TN)
        dq[i] = (dquery * valid).astype(bf16)
        dkl[i] = fold(dot(ds, q_ref[i]))
        bands = [toeplitz(small[i, 4 + head : 5 + head, 0:GROUP]) for head in range(3)]
        high = jnp.concatenate(bands, axis=0).astype(bf16)
        gram = jnp.zeros((384, GROUP), f32)
        for block in range(count // 128):
            conv = dot(high, dctx[block * 128 : block * 128 + 256].astype(bf16))
            dv[i, block * 128 : block * 128 + 128] = head_select(conv, 128)
            piece = dctx[HALO + block * 128 : HALO + block * 128 + 128]
            stacked = jnp.concatenate([jnp.where(lane == head, piece, 0.0) for head in range(3)], axis=0)
            gram = gram + dot(stacked.astype(bf16), v_ref[i, block * 128 : block * 128 + 256], NT)
        dtaps[i] = jnp.zeros((8, GROUP), f32)
        for head in range(3):
            part_high, part_low = split(gram[head * 128 : head * 128 + 128])
            upturned = dot(flip, part_high) + dot(flip, part_low)
            straight = pltpu.roll(upturned, GROUP - 127, 1, stride=1, stride_axis=0)
            summed = jnp.sum(straight, axis=0, keepdims=True)
            dtaps[i, 1 + head : 2 + head, :] = jnp.where(iota((1, GROUP), 1) < TAPS, summed, 0.0)
        return 0

    lax.fori_loop(0, 4, body, 0)


def third_back_kernel(info, x0, x1, lm, wst, k_ref, v_ref, dvc, dq, dkl, ctx, joint, send, partial):
    count = k_ref.shape[1]
    valid = (rows_of(info, count, 0) < info[0]).astype(f32)
    none = jnp.zeros((64, 1), f32)

    def body(i, _):
        dx = spread(x0[i] + x1[i ^ 1])
        dweight = mm(spread(lm[i, :, 2 * GROUP : 3 * GROUP]), dx, TN)
        stats = wst[i]
        weight = spread(jnp.where(iota((64, GROUP), 1) < 192, stats, 0.0))
        inner = jnp.sum(dweight * weight, axis=1, keepdims=True)
        top = jnp.concatenate([stats[:, 192 + head : 193 + head] for head in range(3)] + [none], axis=0)
        total = jnp.concatenate([stats[:, 196 + head : 197 + head] for head in range(3)] + [none + 1.0], axis=0)
        scores = third_scores(info, lm, k_ref, i)
        third = jnp.exp(scores - top) / total
        dw_high = dweight.astype(bf16)
        values = v_ref[i, HALO : HALO + count]
        dthird = dot(dw_high, values, NT)
        ds = (third * (dthird - inner) * 0.125).astype(bf16)
        queries = (spread(lm[i, :, 0:GROUP])).astype(bf16)
        dkey = dot(ds, queries, TN)
        partial[i, :, 0:GROUP] = fold(dot(ds, k_ref[i]))
        partial[i, :, GROUP : 2 * GROUP] = dkl[i]
        dvalues = dot(third.astype(bf16), dw_high, TN)
        joint[i, :, 0:GROUP] = dq[i]
        joint[i, :, GROUP : 2 * GROUP] = (dkey * valid).astype(bf16)
        joint[i, :, 2 * GROUP : 3 * GROUP] = ((dvalues + dvc[i]) * valid).astype(bf16)

        @pl.when(i >= 2)
        def _():
            send[i - 2, :, 0 : 3 * GROUP] = joint[i]
            send[i - 2, :, 3 * GROUP : 4 * GROUP] = ctx[i]

        return 0

    lax.fori_loop(0, 4, body, 0)


def token_back_kernel(info, l0, l1, joint, dres, w0, w1, w2, w3, w4, w5, out, held, sems):
    copies = split_copies((w0, w1, w2, w3, w4, w5), PROJECTION, held, sems, info[2])
    start(copies)
    zero_gaps(held, 3)
    count = joint.shape[1]
    mark = iota((1, 64), 1)
    low = (mark * info[0]) >> 6
    high = ((mark + 1) * info[0]) >> 6
    pos = rows_of(info, count, 0)
    member = ((pos >= low) & (pos < high)).astype(bf16)
    row = iota((64, 1), 0)
    width = ((((row + 1) * info[0]) >> 6) - ((row * info[0]) >> 6)).astype(f32)
    out[...] = dres[...]

    def body(i, pooled):
        wait(copies, i)
        out[...] += dot(joint[i], held[i])
        marks = (l0[i].astype(f32) + l1[i ^ 1].astype(f32)) / width
        return pooled + mm_left(marks, held[i, 0 : 2 * GROUP])

    pooled = lax.fori_loop(0, 4, body, jnp.zeros((64, out.shape[1]), f32))
    pooled_high, pooled_low = split(pooled)
    out[...] += dot(member, pooled_high) + dot(member, pooled_low)


def moments(x):
    centered = x - jnp.mean(x, axis=-1, keepdims=True)
    variance = jnp.mean(centered * centered, axis=-1, keepdims=True)
    inverse = lax.rsqrt(variance + 1e-05)
    return centered * inverse, inverse


def attended_kernel(info, ctx, tokens, gain, shift, o0, o1, o2, o3, o4, o5, pre, normed, low, held, sems):
    copies = split_copies((o0, o1, o2, o3, o4, o5), ((0, 192, 0),), held, sems, info[2])
    start(copies)
    zero_gaps(held, 1)
    pre[...] = tokens[...].astype(f32)

    def body(i, _):
        wait(copies, i)
        pre[...] += dot(ctx[i], held[i])
        return 0

    lax.fori_loop(0, 4, body, 0)
    unit, _ = moments(pre[...])
    result = unit * gain[...] + shift[...]
    normed[...] = result
    low[...] = result.astype(bf16)


def gelu_parts(u):
    cdf = 0.5 + 0.5 * lax.erf(u * 0.7071067811865476)
    pdf = jnp.exp(u * u * -0.5) * 0.3989422804014327
    return u * cdf, cdf + u * pdf


def up_kernel(info, low, small, w0, w1, w2, w3, w4, w5, hidden, slope, send, held, sems):
    copies = split_copies((w0, w1, w2, w3, w4, w5), ((192, held.shape[1], 0),), held, sems, info[2])
    start(copies)

    def body(i, _):
        wait(copies, i)
        for chunk in range(3):
            at = slice(chunk * 256, chunk * 256 + 256)
            upward = dot(low[...], held[i, :, at]) + small[i, 0:1, at]
            value, derivative = gelu_parts(upward)
            hidden[i, :, at] = value.astype(bf16)
            slope[i, :, at] = derivative.astype(bf16)

        @pl.when(i >= 2)
        def _():
            send[i - 2] = hidden[i]

        return 0

    send[2] = low[...]
    lax.fori_loop(0, 4, body, 0)


def norm_back(g, gain, unit, inverse):
    scaled = g * gain
    mean1 = jnp.mean(scaled, axis=-1, keepdims=True)
    mean2 = jnp.mean(scaled * unit, axis=-1, keepdims=True)
    return (scaled - mean1 - unit * mean2) * inverse


def down_kernel(info, hidden, normed, grad, gain, shift, w0, w1, w2, w3, w4, w5, out, dsum, dlow, sums, held, sems, acc):
    copies = split_copies((w0, w1, w2, w3, w4, w5), ((0, held.shape[1], 0),), held, sems, info[2])
    start(copies)
    acc[...] = normed[...]

    def body(i, _):
        wait(copies, i)
        acc[...] += dot(hidden[i], held[i])
        return 0

    lax.fori_loop(0, 4, body, 0)
    unit, inverse = moments(acc[...])
    out[...] = (unit * gain[...] + shift[...]).astype(bf16)
    g = grad[...].astype(f32)
    back = norm_back(g, gain[...], unit, inverse)
    dsum[...] = back
    dlow[...] = back.astype(bf16)
    sums[...] = jnp.zeros_like(sums)
    sums[0:1] = jnp.sum(g * unit, axis=0, keepdims=True)
    sums[1:2] = jnp.sum(g, axis=0, keepdims=True)


def hidden_back_kernel(info, dlow, slope, w0, w1, w2, w3, w4, w5, du, send, sums, held, sems):
    copies = split_copies((w0, w1, w2, w3, w4, w5), ((0, held.shape[1], 0),), held, sems, info[2])
    start(copies)
    sums[...] = jnp.zeros_like(sums)

    def body(i, _):
        wait(copies, i)
        for chunk in range(3):
            at = slice(chunk * 256, chunk * 256 + 256)
            back = dot(dlow[...], held[i, at, :], NT) * slope[i, :, at].astype(f32)
            back = back.astype(bf16)
            du[i, :, at] = back
            sums[i, 0:1, at] = jnp.sum(back.astype(f32), axis=0, keepdims=True)

        @pl.when(i >= 2)
        def _():
            send[i - 2] = du[i]

        return 0

    send[2] = dlow[...]
    lax.fori_loop(0, 4, body, 0)


def residual_back_kernel(info, du, dsum, pre, gain, w0, w1, w2, w3, w4, w5, dres, dlow, sums, held, sems, acc):
    copies = split_copies((w0, w1, w2, w3, w4, w5), ((192, held.shape[1], 0),), held, sems, info[2])
    start(copies)
    acc[...] = dsum[...]

    def body(i, _):
        wait(copies, i)
        acc[...] += dot(du[i], held[i], NT)
        return 0

    lax.fori_loop(0, 4, body, 0)
    unit, inverse = moments(pre[...])
    g = acc[...]
    back = norm_back(g, gain[...], unit, inverse)
    dres[...] = back
    dlow[...] = back.astype(bf16)
    sums[...] = jnp.zeros_like(sums)
    sums[0:1] = jnp.sum(g * unit, axis=0, keepdims=True)
    sums[1:2] = jnp.sum(g, axis=0, keepdims=True)


def feed_grad_kernel(
    pick, hidden, hidden_other, gd, du_other, du, low, down0, down1, up0, up1, left, right, sems
):
    half = left.shape[-1]
    copies = []

    def bring(source, target):
        copy = pltpu.make_async_copy(source, target, sems.at[len(copies)])
        copy.start()
        copies.append(copy)

    for part, sources in ((0, (hidden.at[0], hidden_other.at[0], hidden.at[1], hidden_other.at[1])), (1, (low, hidden_other.at[2]))):
        columns = pl.ds(pl.multiple_of(pick[part] * half, half), half)
        for n, source in enumerate(sources):
            bring(source.at[:, columns], left.at[4 * part + n])
        if part == 0:
            bring(gd, right.at[0])
            bring(du_other.at[2], right.at[1])
        else:
            for j in range(2):
                bring(du.at[j], right.at[2 + 2 * j])
                bring(du_other.at[j], right.at[3 + 2 * j])
    for copy in copies[:6]:
        copy.wait()

    def body(n, _):
        @pl.when(n == 2)
        def _():
            for copy in copies[6:]:
                copy.wait()

        down = n < 2
        at_left = jnp.where(down, 2 * n, 4)
        at_right = jnp.where(down, 0, 2 * n - 2)
        total = dot(left[at_left], right[at_right], TN) + dot(left[at_left + 1], right[at_right + 1], TN)
        total = total.astype(bf16)
        for k, out in enumerate((down0, down1, up0, up1)):

            @pl.when(n == k)
            def _():
                out[...] = total

        return 0

    lax.fori_loop(0, 4, body, 0)


def feed_grad(pick, hidden, hidden_other, gd, du_other, du, low):
    count, width = gd.shape
    return (
        feed_grad_kernel,
        [((width // 2, width), bf16)] * 4,
        [(VMEM, pick.astype(jnp.int32))] + [(ANY, x) for x in (hidden, hidden_other, gd, du_other, du, low)],
        [
            pltpu.VMEM((6, count, width // 2), bf16),
            pltpu.VMEM((6, count, width), bf16),
            pltpu.SemaphoreType.DMA((12,)),
        ],
        (0,),
    )


def joint_grad_kernel(joint, other, ctx, tokens, tokens_other, g, g_other, first, second):
    def body(kind, _):
        at = pl.ds(pl.multiple_of(kind * GROUP, GROUP), GROUP)
        total = dot(joint[0, :, at], tokens[...], TN) + dot(other[0, :, at], tokens_other[...], TN)
        total = total[0:192].astype(bf16)

        @pl.when(kind < 2)
        def _():
            first[pl.ds(pl.multiple_of(kind * 192, 192), 192)] = total

        @pl.when(kind == 2)
        def _():
            second[0:192] = total

        return 0

    lax.fori_loop(0, 3, body, 0)
    total = dot(ctx[0], g[...], TN) + dot(other[0, :, 3 * GROUP : 4 * GROUP], g_other[...], TN)
    second[192:384] = total[0:192].astype(bf16)


def joint_grad(joint, other, ctx, tokens, tokens_other, g, g_other, block, name):
    count, width = tokens.shape
    whole = pl.BlockSpec((count, width), lambda j: (0, 0))
    return pl.pallas_call(
        joint_grad_kernel,
        grid=(1,),
        out_shape=[jax.ShapeDtypeStruct((width // 2, width), bf16)] * 2,
        in_specs=[
            pl.BlockSpec((1, count, 3 * GROUP), lambda j: (block, 0, 0)),
            pl.BlockSpec((1, count, 4 * GROUP), lambda j: (block, 0, 0)),
            pl.BlockSpec((1, count, GROUP), lambda j: (block, 0, 0)),
            whole,
            whole,
            whole,
            whole,
        ],
        out_specs=[pl.BlockSpec((width // 2, width), lambda j: (0, 0))] * 2,
        compiler_params=pltpu.CompilerParams(vmem_limit_bytes=40 << 20),
        cost_estimate=pl.CostEstimate(flops=16 * count * GROUP * width, bytes_accessed=8 << 20, transcendentals=0),
        name=name,
    )(joint, other, ctx, tokens, tokens_other, g, g_other)


HOP = {1: 2, 2: 1, 3: 3}


def hop(x, step):
    return lax.ppermute(x, "head", [(i, i ^ HOP[step]) for i in range(4)])


def after(x, *deps):
    return lax.optimization_barrier((x,) + deps)[0]


def local(
    batch_count,
    tokens,
    lengths,
    w_query,
    w_key,
    w_value,
    w_out,
    conv_taps,
    w_up,
    b_up,
    w_down,
    gain_attn,
    shift_attn,
    gain_ffn,
    shift_ffn,
    grad_out,
):
    tokens = tokens[0]
    grad_out = grad_out[0]
    count, width = tokens.shape
    ext = count + 128
    length = lengths[0]
    place = lax.axis_index("head")
    batch = lax.axis_index("batch")
    core = place & 1
    side = batch & 1
    info = jnp.stack([length, place * count, side]).astype(jnp.int32)
    gain_attn, shift_attn, gain_ffn, shift_ffn = (
        x.reshape(1, width) for x in (gain_attn, shift_attn, gain_ffn, shift_ffn)
    )
    vm, an = VMEM, ANY

    def hop_batch(x, step):
        return lax.ppermute(x, "batch", [(i, i ^ step) for i in range(batch_count)])

    def neighbours(x, other):
        first = core == 0
        far = lax.ppermute(jnp.where(first, x[:HALO], x[-HALO:]), "head", [(1, 2), (2, 1)])
        return jnp.where(first, far, other[-HALO:]), jnp.where(first, other[:HALO], far)

    marks = jnp.arange(LANDMARKS + 1, dtype=jnp.int32) * length // LANDMARKS
    positions = info[1] + jnp.arange(count, dtype=jnp.int32)
    member = (positions[None, :] >= marks[:-1, None]) & (positions[None, :] < marks[1:, None])
    pooled = jnp.dot(member.astype(bf16), tokens, preferred_element_type=f32)
    pooled = (pooled / (marks[1:] - marks[:-1]).astype(f32)[:, None]).astype(bf16)
    pools = [pooled] + [hop(pooled, n) for n in (1, 2, 3)]

    taps = jnp.pad(conv_taps, ((0, 0), (0, width - TAPS)))
    taps_back = jnp.pad(conv_taps[:, ::-1], ((0, 0), (0, width - TAPS)))
    small_own = jnp.concatenate([b_up[None], taps, taps_back, jnp.zeros((1, width), f32)], axis=0)
    term1 = small_own.astype(bf16)
    rest = small_own - lax.reduce_precision(small_own, 8, 7)
    term2 = rest.astype(bf16)
    term3 = (rest - lax.reduce_precision(rest, 8, 7)).astype(bf16)
    wt_own = jnp.concatenate(
        [w_query.T, w_key.T, w_value.T, term1, term2, term3, jnp.zeros((8, width), bf16)], axis=0
    )
    tokens_other = hop(tokens, 2)
    before, behind = neighbours(tokens, tokens_other)

    def column_half(own):
        return lax.dynamic_slice_in_dim(own, side * (width // 2), width // 2, 1)

    wt_other = hop(wt_own, 2)
    wt_across = hop(after(column_half(wt_own), *pools), 1)
    lm_own, pooled_low, iterates = call(
        landmark_kernel,
        [((64, 3 * GROUP), f32), ((64, width), bf16), ((NEWTON, 4, 3, 64, 64), f32)],
        [(vm, x) for x in pools] + [(vm, wt_own)],
        flops=int(1e9),
        size=4 << 20,
        name="landmarks",
    )
    lm_own = after(lm_own, wt_across, before, behind)
    lm_across = hop(lm_own, 1)
    wt_across_x = hop_batch(after(wt_across, pooled_low), 1)
    lm = jnp.stack([lm_own, lm_across, hop(lm_own, 2), hop(lm_across, 2)])
    wt = [wt_own, wt_across, wt_across_x, wt_other, hop(wt_across, 2), hop(wt_across_x, 2)]

    def small_of(block):
        return sum(block[576 + 8 * n : 584 + 8 * n].astype(f32) for n in range(3))

    def small_joined(near, far):
        near, far = small_of(near), small_of(far)
        first = side == 0
        return jnp.concatenate([jnp.where(first, near, far), jnp.where(first, far, near)], axis=1)

    small = jnp.stack(
        [small_of(wt[0]), small_joined(wt[1], wt[2]), small_of(wt[3]), small_joined(wt[4], wt[5])]
    )
    out_up_own = jnp.concatenate([w_out, after(w_up, pooled)], axis=0)
    out_up_across = hop(after(column_half(out_up_own), lm_across), 1)
    down_across = hop(after(column_half(w_down), lm_across), 1)
    q, k, v = call(
        project_kernel,
        [((4, count, GROUP), bf16), ((4, count, GROUP), bf16), ((4, ext, GROUP), bf16)],
        [(vm, info), (vm, tokens), (vm, before), (vm, behind)] + [(an, w) for w in wt],
        [pltpu.VMEM((4, 3 * GROUP, width), bf16), pltpu.SemaphoreType.DMA((4, 3, 2))],
        flops=2 * count * width * 3072,
        size=8 << 20,
        smem=(0,),
        name="project",
    )
    out_up_across_x = hop_batch(after(out_up_across, q), 1)
    (pay,) = call(
        third_kernel,
        [((4, 64, GROUP), bf16)],
        [(vm, info), (vm, lm), (vm, k), (vm, v)],
        flops=int(1e9),
        size=3 << 20,
        smem=(0,),
        name="third",
    )
    pays = [pay, hop(pay, 1), hop(pay, 2), hop(pay, 3)]
    ctx, wst, x_mid = call(
        context_kernel,
        [((4, count, GROUP), bf16), ((4, 64, GROUP), f32), ((4, 64, GROUP), f32)],
        [(vm, p) for p in pays] + [(vm, lm), (vm, q), (vm, v), (vm, small)],
        flops=int(3e9),
        size=5 << 20,
        name="context",
    )
    out_up_far = after((out_up_across, out_up_across_x), ctx)
    out_up = [out_up_across, out_up_across_x, hop(after(out_up_own, q), 2), hop(out_up_far[0], 2), hop(out_up_far[1], 2)]
    down_across_x = hop_batch(after(down_across, ctx), 1)
    wo = [(an, w) for w in [w_out] + out_up]
    wu = [(an, w) for w in [w_up] + out_up]
    out_scratch = [pltpu.VMEM((4, GROUP, width), bf16), pltpu.SemaphoreType.DMA((4, 1, 2))]
    wide = [pltpu.VMEM((4, width, width), bf16), pltpu.SemaphoreType.DMA((4, 1, 2))]
    acc = [pltpu.VMEM((count, width), f32)]

    pre, normed, normed_low = call(
        attended_kernel,
        [((count, width), f32), ((count, width), f32), ((count, width), bf16)],
        [(vm, info), (vm, ctx), (vm, tokens), (vm, gain_attn), (vm, shift_attn)] + wo,
        out_scratch,
        flops=2 * count * width * width,
        size=6 << 20,
        smem=(0,),
        name="attended",
    )
    down_far = after((down_across, down_across_x), normed_low)
    down = [down_across, down_across_x, hop(after(w_down, ctx), 2), hop(down_far[0], 2), hop(down_far[1], 2)]
    wd = [(an, w) for w in [w_down] + down]
    hidden, slope, hidden_send = call(
        up_kernel,
        [((4, count, width), bf16), ((4, count, width), bf16), ((3, count, width), bf16)],
        [(vm, info), (vm, normed_low), (vm, small)] + wu,
        wide,
        flops=2 * count * width * 3072,
        size=12 << 20,
        smem=(0,),
        name="up",
    )
    hidden_other = hop(hidden_send, 2)
    output, d_sum, gd, sums_ffn = call(
        down_kernel,
        [((count, width), bf16), ((count, width), f32), ((count, width), bf16), ((8, width), f32)],
        [(vm, info), (vm, hidden), (vm, normed), (vm, grad_out), (vm, gain_ffn), (vm, shift_ffn)] + wd,
        wide + acc,
        flops=2 * count * width * 3072,
        size=14 << 20,
        smem=(0,),
        name="down",
    )

    steps = [1 << n for n in range(batch_count.bit_length() - 1)]
    down_order = steps[:2] + ["y"] + steps[2:]
    up_order = steps[1:2] + steps[:1] + ["y"] + steps[2:]

    def bit(step):
        return (batch // step) & 1

    def send(x, step):
        return hop(x, 1) if step == "y" else hop_batch(x, step)

    def chain(pieces, step):
        received = [send(pieces[0], step)]
        for piece in pieces[1:]:
            received.append(send(after(piece, received[-1]), step))
        return received

    def add_all(kept, received):
        return [(a.astype(f32) + b.astype(f32)).astype(bf16) for a, b in zip(kept, received)]

    def split_for(pieces, step):
        if step == "y":
            return pieces[:1], pieces[1:]
        rows = pieces[0].shape[0] // 2
        kept = [lax.dynamic_slice_in_dim(x, bit(step) * rows, rows, 0) for x in pieces]
        sent = [lax.dynamic_slice_in_dim(x, (1 - bit(step)) * rows, rows, 0) for x in pieces]
        if len(pieces) > 1:
            sent = [jnp.stack(sent)]
        return kept, sent

    def exchange(pieces, step):
        kept, sent = split_for(pieces, step)
        received = send(sent[0], step)
        return kept, [received] if received.ndim == 2 else [received[n] for n in range(len(kept))]

    def grow(x, step):
        other = hop_batch(x, step)
        mine_last = bit(step) == 1
        return jnp.concatenate([jnp.where(mine_last, other, x), jnp.where(mine_last, x, other)], axis=0)

    def grow_first(x, step):
        return [x[0], hop_batch(x[0][: x[0].shape[0] // 2], step)]

    def grow_second(x, step):
        own, other = x
        other = jnp.concatenate([other, hop_batch(own[own.shape[0] // 2 :], step)], axis=0)
        mine_last = bit(step) == 1
        return [jnp.concatenate([jnp.where(mine_last, other, own), jnp.where(mine_last, own, other)], axis=0)]

    def in_two(task, order):
        return task[:-1] + [lambda x: x] * IDLE + [lambda x: grow_first(x, order[0]), lambda x: grow_second(x, order[0])]

    def rest_of(order, done):
        back = [step for step in order if step != "y"][::-1]
        return [lambda x, step=step: add_all(*exchange(x, step)) for step in order[done:]] + [
            lambda x, step=step: [grow(x[0], step)] for step in back
        ]

    du, du_send, sums_up = call(
        hidden_back_kernel,
        [((4, count, width), bf16), ((3, count, width), bf16), ((4, 8, width), f32)],
        [(vm, info), (vm, gd), (vm, slope)] + wd,
        wide,
        flops=2 * count * width * 3072,
        size=12 << 20,
        smem=(0,),
        name="hidden_back",
    )
    du_other = hop(du_send, 2)
    mine = jnp.stack([bit(down_order[0]), bit(up_order[0])])
    operands = (hidden, hidden_other, gd, du_other, du, normed_low)
    ((down_sent0, down_sent1, up_sent0, up_sent1),) = call_many([feed_grad(1 - mine, *operands)], "grad_sent")
    down_first = send(down_sent0, down_order[0])
    up_first = send(up_sent0, up_order[0])
    kept, (d_res, ga, sums_attn) = call_many(
        [
            feed_grad(mine, hidden, hidden_other, after(gd, down_sent0), du_other, du, normed_low),
            (
                residual_back_kernel,
                [((count, width), f32), ((count, width), bf16), ((8, width), f32)],
                [(vm, info), (vm, du), (vm, d_sum), (vm, pre), (vm, gain_attn)] + wu,
                wide + acc,
                (0,),
            ),
        ],
        "grad_kept",
    )
    down_kept, up_kept = kept[:2], kept[2:]
    ga, down_first, up_first = after((ga, down_first, up_first), d_res)
    ga_other = hop(ga, 2)
    ga_before, ga_behind = neighbours(ga, ga_other)
    down_second = send(after(down_sent1, down_first), down_order[0])
    up_second = send(after(up_sent1, up_first), up_order[0])
    dx, dq, dkl, dv_conv, dtaps = call(
        first_back_kernel,
        [
            ((4, 64, GROUP), f32),
            ((4, count, GROUP), bf16),
            ((4, 64, GROUP), f32),
            ((4, count, GROUP), f32),
            ((4, 8, GROUP), f32),
        ],
        [(vm, info), (vm, after(ga, down_first, up_first)), (vm, ga_before), (vm, ga_behind)]
        + wo
        + [(vm, lm), (vm, q), (vm, v), (vm, small), (vm, x_mid)],
        out_scratch + [pltpu.VMEM((ext, width), bf16), pltpu.VMEM((ext, GROUP), f32)],
        flops=int(5e9),
        size=10 << 20,
        smem=(0,),
        name="first_back",
    )

    def swap_core(x):
        other = hop(x, 2)
        return x.astype(f32) + jnp.concatenate([other[2:4], other[0:2]], axis=0).astype(f32)

    dx, down_second, up_second = after((dx, down_second, up_second), dtaps)
    dx = swap_core(after(dx, down_second, up_second))
    down_sent, up_sent = [down_first, down_second], [up_first, up_second]
    d_down = exchange(add_all(down_kept, down_sent), down_order[1])
    d_up = exchange(add_all(up_kept, up_sent), up_order[1])
    dx_across = hop(dx, 1)
    dx, dx_across, d_down, d_up = after((dx, dx_across, d_down, d_up), dx_across)
    d_down = exchange(add_all(*d_down), down_order[2])
    d_up = exchange(add_all(*d_up), up_order[2])
    dx, dx_across = after((dx, dx_across), d_down[0], d_up[0])
    joint, joint_send, partial = call(
        third_back_kernel,
        [((4, count, 3 * GROUP), bf16), ((2, count, 4 * GROUP), bf16), ((4, 64, 2 * GROUP), f32)],
        [(vm, info), (vm, dx), (vm, dx_across), (vm, lm), (vm, wst), (vm, k), (vm, v), (vm, dv_conv), (vm, dq)]
        + [(vm, dkl), (vm, ctx)],
        flops=int(5e9),
        size=8 << 20,
        smem=(0,),
        name="third_back",
    )
    joint_other = hop(after(joint_send, d_down[1], d_up[1]), 2)
    d_down, d_up = after((d_down, d_up), partial)
    d_down, d_up = add_all(*d_down), add_all(*d_up)
    operands = (after(joint, *d_down, *d_up), joint_other, ctx, tokens, tokens_other, ga, ga_other)
    sent = joint_grad(*operands, 1, "grad_joint_sent")
    joint_first = send(sent[0], "y")
    d_down, d_up = after((d_down, d_up), *sent)
    d_down, d_up = exchange(d_down, down_order[3]), exchange(d_up, up_order[3])
    (partial,) = call(
        inverse_back_kernel,
        [((4, 64, 2 * GROUP), bf16)],
        [(vm, dx), (vm, dx_across), (vm, wst), (vm, lm_own), (vm, iterates), (vm, after(partial, *sent))],
        flops=int(1e9),
        size=4 << 20,
        name="inverse_back",
    )
    partial = after(partial, joint_first, d_down[1], d_up[1])
    d_down, d_up = after((d_down, d_up), partial)
    d_down, d_up = add_all(*d_down), add_all(*d_up)
    partial = swap_core(partial).astype(bf16)
    partial_across = hop(partial, 1)
    down_rest, up_rest = rest_of(down_order, 4), rest_of(up_order, 4)
    if EARLY >= 1:
        d_down, d_up = after((d_down, d_up), partial)
        d_down, d_up = down_rest[0](d_down), up_rest[0](d_up)
        partial, partial_across = after((partial, partial_across), partial_across, d_down[0], d_up[0])
        down_rest, up_rest = down_rest[1:], up_rest[1:]
    else:
        partial, partial_across = after((partial, partial_across), partial_across)
    joint_second = send(after(sent[1], partial_across), "y")
    joint_sent = [joint_first, joint_second]
    joint_kept = joint_grad(*after(operands, partial), 0, "grad_joint_kept")
    if EARLY >= 2:
        d_down, d_up = down_rest[0](d_down), up_rest[0](d_up)
        down_rest, up_rest = down_rest[1:], up_rest[1:]
    (d_tokens,) = call(
        token_back_kernel,
        [((count, width), f32)],
        [(vm, info), (vm, partial), (vm, partial_across), (vm, joint), (vm, d_res)] + [(an, w) for w in wt],
        [pltpu.VMEM((4, 3 * GROUP, width), bf16), pltpu.SemaphoreType.DMA((4, 3, 2))],
        flops=2 * count * width * 3072,
        size=10 << 20,
        smem=(0,),
        name="token_back",
    )
    landmark_own = (partial[0].astype(f32) + partial_across[1].astype(f32)).astype(bf16)
    low_rank = dot(landmark_own, pooled_low, TN)
    low_rank = jnp.concatenate([low_rank[0:192], low_rank[GROUP : GROUP + 192]], axis=0)
    d_first = (joint_kept[0].astype(f32) + joint_sent[0].astype(f32) + low_rank).astype(bf16)
    d_second = (joint_kept[1].astype(f32) + joint_sent[1].astype(f32)).astype(bf16)
    norms = jnp.concatenate([sums_attn[0:2], sums_ffn[0:2]], axis=0)
    dtaps = jnp.pad(dtaps[:, 1:4], ((0, 0), (0, 0), (0, width - GROUP)))
    minor = jnp.concatenate([sums_up[:, 0:1], dtaps, jnp.broadcast_to(norms, (4, 4, width))], axis=1)
    minor = after(minor, joint_second)
    minor = minor[0:2] + hop(minor[2:4], 2)
    minor = minor[0] + hop(minor[1], 1)
    orders = [steps, steps[1:2] + steps[:1] + steps[2:]]
    values = [[d_first], [d_second], d_down, d_up, [minor]]
    tasks = [
        rest_of(orders[0], 0),
        rest_of(orders[1], 0),
        in_two(down_rest, down_order),
        in_two(up_rest, up_order),
        [lambda x: x] * LATE + [lambda x, step=step: [x[0] + hop_batch(x[0], step)] for step in steps],
    ]
    for turn in range(max(len(task) for task in tasks)):
        anchors = (values[0][0], values[1][0]) + ((d_tokens,) if turn == 0 else ())
        if turn == IDLE + 2:
            anchors += (values[2][-1], values[3][-1])
        values = [
            task[turn](after(value, *anchors)) if turn < len(task) else value for value, task in zip(values, tasks)
        ]
    d_parts = [values[0][0].astype(f32), values[1][0].astype(f32)]
    d_w_down, d_w_up = values[2][0].astype(f32), values[3][0].astype(f32)
    minor = values[4][0]
    d_w_query, d_w_key = d_parts[0][0:192].T, d_parts[0][192:384].T
    d_w_value, d_w_out = d_parts[1][0:192].T, d_parts[1][192:384]

    return (
        output[None],
        d_tokens[None],
        d_w_query,
        d_w_key,
        d_w_value,
        d_w_out,
        minor[1:4, 0:TAPS],
        d_w_up,
        minor[0],
        d_w_down,
        minor[4],
        minor[5],
        minor[6],
        minor[7],
    )


def solution(mesh):
    return jax.shard_map(
        functools.partial(local, mesh.shape["batch"]),
        mesh=mesh,
        in_specs=(
            P("batch", "head", None),
            P("batch"),
            P(None, "head"),
            P(None, "head"),
            P(None, "head"),
            P("head", None),
            P("head", None),
            P(None, "head"),
            P("head"),
            P("head", None),
            P(),
            P(),
            P(),
            P(),
            P("batch", "head", None),
        ),
        out_specs=(
            P("batch", "head", None),
            P("batch", "head", None),
            P(None, "head"),
            P(None, "head"),
            P(None, "head"),
            P("head", None),
            P("head", None),
            P(None, "head"),
            P("head"),
            P("head", None),
            P(),
            P(),
            P(),
            P(),
        ),
        check_vma=False,
    )
```

profile of v0, /device:TPU:0, one launch (start us, length us, event | category | flops | bytes accessed | tf_op | source)
XLA Modules:
  0.0 333.3 jit_solution(8216599199930682379)
XLA Ops:
  14.8 8.7 %landmarks.1 = (f32[64,768]{1,0:T(8,128)S(1)}, bf16[64,768]{1,0:T(8,128)(2,1)S(1)}, f32[6,4,3,64,64]{4,3,2,1,0:T(8,128)S(1)}) custom-call(bf16[64,768]{1,0:T(8,128)(2,1)S(1)} %fusion.1.p0, bf16[64,768]{1,0:T(8,128)(2,1)S(1)} %collective-permute-done.p1, bf16[64,768]{1,0:T(8,128)(2,1)S(1)} %collective-permute-done.1.p2, ...), custom_call_target="tpu_custom_call" | custom-call | flops 1000000000 | bytes 4194304 | tf_op jit(solution)/shard_map/landmarks/pallas_call | solution.py:57
  30.1 4.5 %collective-permute-done.6 = f32[64,768]{1,0:T(8,128)S(1)} collective-permute-done((f32[64,768]{1,0:T(8,128)S(1)}, f32[64,768]{1,0:T(8,128)S(1)}, u32[]{:S(2)}, u32[]{:S(2)}) %collective-permute-start.6) | collective-permute-done | bytes 196640 | tf_op jit(solution)/shard_map/ppermute | solution.py:724
  40.7 5.4 %project.1 = (bf16[4,512,256]{2,1,0:T(8,128)(2,1)S(1)}, bf16[4,512,256]{2,1,0:T(8,128)(2,1)S(1)}, bf16[4,640,256]{2,1,0:T(8,128)(2,1)S(1)}) custom-call(s32[3]{0:T(128)S(1)} %pad_add_fusion.info.refs_7_, bf16[512,768]{1,0:T(8,128)(2,1)S(1)} %bitcast.68, bf16[32,768]{1,0:T(8,128)(2,1)S(1)} %get-tuple-element.306.before, ...), custom_call_target="tpu_custom_call" | custom-call | flops 2415919104 | bytes 8388608 | tf_op jit(solution)/shard_map/project/pallas_call | solution.py:57
  46.4 5.9 %collective-permute-done.16.o1.w1.refs_13_ = bf16[960,384]{1,0:T(8,128)(2,1)S(1)} collective-permute-done((bf16[960,384]{1,0:T(8,128)(2,1)S(1)}, bf16[960,384]{1,0:T(8,128)(2,1)S(1)}, u32[]{:S(2)}, u32[]{:S(2)}) %collective-permute-start.16) | collective-permute-done | bytes 737312 | tf_op jit(solution)/shard_map/ppermute | solution.py:724
  52.6 4.2 %third.1.p0 = bf16[4,64,256]{2,1,0:T(8,128)(2,1)S(1)} custom-call(s32[3]{0:T(128)S(1)} %pad_add_fusion.info.refs_7_, f32[4,64,768]{2,1,0:T(8,128)S(1)} %pad_maximum_fusion.lm, bf16[4,512,256]{2,1,0:T(8,128)(2,1)S(1)} %get-tuple-element.153.k_ref, bf16[4,640,256]{2,1,0:T(8,128)(2,1)S(1)} %get-tuple-element.154.v_ref), custom_call_target="tpu_custom_call" | custom-call | flops 1000000000 | bytes 3145728 | tf_op jit(solution)/shard_map/third/pallas_call | solution.py:57
  64.9 6.7 %context.1 = (bf16[4,512,256]{2,1,0:T(8,128)(2,1)S(1)}, f32[4,64,256]{2,1,0:T(8,128)S(1)}, f32[4,64,256]{2,1,0:T(8,128)S(1)}) custom-call(bf16[4,64,256]{2,1,0:T(8,128)(2,1)S(1)} %third.1.p0, bf16[4,64,256]{2,1,0:T(8,128)(2,1)S(1)} %collective-permute-done.13.p1, bf16[4,64,256]{2,1,0:T(8,128)(2,1)S(1)} %collective-permute-done.14.p2, ...), custom_call_target="tpu_custom_call" | custom-call | flops 3000000000 | bytes 5242880 | tf_op jit(solution)/shard_map/context/pallas_call | solution.py:57
  73.0 4.9 %collective-permute-done.21.w1 = bf16[768,384]{1,0:T(8,128)(2,1)S(1)} collective-permute-done((bf16[768,384]{1,0:T(8,128)(2,1)S(1)}, bf16[768,384]{1,0:T(8,128)(2,1)S(1)}, u32[]{:S(2)}, u32[]{:S(2)}) %collective-permute-start.21) | collective-permute-done | bytes 589856 | tf_op jit(solution)/shard_map/ppermute | solution.py:724
  83.0 9.0 %collective-permute-done.22.w2 = bf16[768,384]{1,0:T(8,128)(2,1)S(1)} collective-permute-done((bf16[768,384]{1,0:T(8,128)(2,1)S(1)}, bf16[768,384]{1,0:T(8,128)(2,1)S(1)}, u32[]{:S(2)}, u32[]{:S(2)}) %collective-permute-start.22) | collective-permute-done | bytes 589856 | tf_op jit(solution)/shard_map/ppermute | solution.py:765
  92.7 8.7 %up.1 = (bf16[4,512,768]{2,1,0:T(8,128)(2,1)S(1)}, bf16[4,512,768]{2,1,0:T(8,128)(2,1)}, bf16[3,512,768]{2,1,0:T(8,128)(2,1)}) custom-call(s32[3]{0:T(128)S(1)} %pad_add_fusion.info.refs_7_, bf16[512,768]{1,0:T(8,128)(2,1)S(1)} %get-tuple-element.163.low.refs_6_, f32[4,8,768]{2,1,0:T(8,128)S(1)} %pad_maximum_fusion.11.small, ...), custom_call_target="tpu_custom_call" | custom-call | flops 2415919104 | bytes 12582912 | tf_op jit(solution)/shard_map/up/pallas_call | solution.py:57
  101.6 6.5 %down.1 = (bf16[512,768]{1,0:T(8,128)(2,1)}, f32[512,768]{1,0:T(8,128)S(1)}, bf16[512,768]{1,0:T(8,128)(2,1)S(1)}, f32[8,768]{1,0:T(8,128)S(1)}) custom-call(s32[3]{0:T(128)S(1)} %pad_add_fusion.info.refs_7_, bf16[4,512,768]{2,1,0:T(8,128)(2,1)S(1)} %get-tuple-element.164.hidden.refs_1_, f32[512,768]{1,0:T(8,128)S(1)} %get-tuple-element.165.normed, ...), custom_call_target="tpu_custom_call" | custom-call | flops 2415919104 | bytes 14680064 | tf_op jit(solution)/shard_map/down/pallas_call | solution.py:57
  109.2 6.4 %hidden_back.1 = (bf16[4,512,768]{2,1,0:T(8,128)(2,1)S(1)}, bf16[3,512,768]{2,1,0:T(8,128)(2,1)}, f32[4,8,768]{2,1,0:T(8,128)S(1)}) custom-call(s32[3]{0:T(128)S(1)} %pad_add_fusion.info.refs_7_, bf16[512,768]{1,0:T(8,128)(2,1)S(1)} %get-tuple-element.178.dlow.refs_3_, bf16[4,512,768]{2,1,0:T(8,128)(2,1)S(1)} %copy-done.73, bf16[768,768]{1,0:T(8,128)(2,1)S(1)} %copy-done.30, ...), custom_call_target="tpu_custom_call" | custom-call | flops 2415919104 | bytes 12582912 | tf_op jit(solution)/shard_map/hidden_back/pallas_call | solution.py:57
  118.4 4.4 %collective-permute-done.27.refs_4_ = bf16[3,512,768]{2,1,0:T(8,128)(2,1)} collective-permute-done((bf16[3,512,768]{2,1,0:T(8,128)(2,1)}, bf16[3,512,768]{2,1,0:T(8,128)(2,1)}, u32[]{:S(2)}, u32[]{:S(2)}) %collective-permute-start.27) | collective-permute-done | bytes 2359328 | tf_op jit(solution)/shard_map/ppermute | solution.py:724
  125.1 7.1 %grad_sent.1 = (bf16[384,768]{1,0:T(8,128)(2,1)}, bf16[384,768]{1,0:T(8,128)(2,1)S(1)}, bf16[384,768]{1,0:T(8,128)(2,1)}, bf16[384,768]{1,0:T(8,128)(2,1)S(1)}) custom-call(s32[2]{0:T(128)S(1)} %get-tuple-element.287.refs_0_, bf16[4,512,768]{2,1,0:T(8,128)(2,1)} %copy-done.1, bf16[3,512,768]{2,1,0:T(8,128)(2,1)} %collective-permute-done.26.refs_2_, ...), custom_call_target="tpu_custom_call" | custom-call | flops 5000000000 | bytes 10485760 | tf_op jit(solution)/shard_map/grad_sent/pallas_call | solution.py:57
  136.1 15.2 %grad_kept.1 = (bf16[384,768]{1,0:T(8,128)(2,1)S(1)}, bf16[384,768]{1,0:T(8,128)(2,1)S(1)}, bf16[384,768]{1,0:T(8,128)(2,1)S(1)}, bf16[384,768]{1,0:T(8,128)(2,1...) custom-call(s32[2]{0:T(128)S(1)} %get-tuple-element.288.refs_0_, ...), custom_call_target="tpu_custom_call" | custom-call | flops 5000000000 | bytes 10485760 | tf_op jit(solution)/shard_map/grad_kept/pallas_call | solution.py:57
  157.5 9.4 %first_back.1 = (f32[4,64,256]{2,1,0:T(8,128)S(1)}, bf16[4,512,256]{2,1,0:T(8,128)(2,1)S(1)}, f32[4,64,256]{2,1,0:T(8,128)S(1)}, f32[4,512,256]{2,1,0:T(8,128)S(1)}, f32[4,8,256]{2,1,0:T(8,128)S(1)}) custom-call(s32[3]{0:T(128)S(1)} %pad_add_fusion.info.refs_7_, bf16[512,768]{1,0:T(8,128)(2,1)S(1)} %get-tuple-element.248.g_ref.g, ...), custom_call_target="tpu_custom_call" | custom-call | flops 5000000000 | bytes 10485760 | tf_op jit(solution)/shard_map/first_back/pallas_call | solution.py:57
  174.1 11.3 %collective-permute-done.36 = bf16[2,192,768]{2,1,0:T(8,128)(2,1)S(1)} collective-permute-done((bf16[2,192,768]{2,1,0:T(8,128)(2,1)S(1)}, bf16[2,192,768]{2,1,0:T(8,128)(2,1)S(1)}, u32[]{:S(2)}, u32[]{:S(2)}) %collective-permute-start.36) | collective-permute-done | bytes 589856 | tf_op jit(solution)/shard_map/ppermute | solution.py:765
  189.6 4.9 %third_back.1 = (bf16[4,512,768]{2,1,0:T(8,128)(2,1)S(1)}, bf16[2,512,1024]{2,1,0:T(8,128)(2,1)S(1)}, f32[4,64,512]{2,1,0:T(8,128)S(1)}) custom-call(s32[3]{0:T(128)S(1)} %pad_add_fusion.info.refs_7_, f32[4,64,256]{2,1,0:T(8,128)S(1)} %maximum_add_fusion.1.x0, f32[4,64,256]{2,1,0:T(8,128)S(1)} %collective-permute-done.35.x1, f32[4,64,768]{2,1,0:T(8,128)S(1)} %copy-done.44, ...), custom_call_target="tpu_custom_call" | custom-call | flops 5000000000 | bytes 8388608 | tf_op jit(solution)/shard_map/third_back/pallas_call | solution.py:57
  197.4 4.2 %collective-permute-done.38 = bf16[192,768]{1,0:T(8,128)(2,1)S(1)} collective-permute-done((bf16[192,768]{1,0:T(8,128)(2,1)S(1)}, bf16[192,768]{1,0:T(8,128)(2,1)S(1)}, u32[]{:S(2)}, u32[]{:S(2)}) %collective-permute-start.38) | collective-permute-done | bytes 294944 | tf_op jit(solution)/shard_map/ppermute | solution.py:724
  224.7 9.4 %inverse_back.1 = bf16[4,64,512]{2,1,0:T(8,128)(2,1)S(1)} custom-call(f32[4,64,256]{2,1,0:T(8,128)S(1)} %maximum_add_fusion.1.x0, f32[4,64,256]{2,1,0:T(8,128)S(1)} %copy-done.60, f32[4,64,256]{2,1,0:T(8,128)S(1)} %copy-done.58, f32[64,768]{1,0:T(8,128)S(1)} %copy-done.42, f32[6,4,3,64,64]{4,3,2,1,0:T(8,128)S(1)} %copy-done.32, f32[4,64,512]{2,1,0:T(8,128)S(1)} %copy-done.47), custom_call_target="tpu_custom_call" | custom-call | flops 1000000000 | bytes 4194304 | tf_op jit(solution)/shard_map/inverse_back/pallas_call | solution.py:57
  239.6 10.2 %collective-permute-done.46 = bf16[96,768]{1,0:T(8,128)(2,1)S(1)} collective-permute-done((bf16[96,768]{1,0:T(8,128)(2,1)S(1)}, bf16[96,768]{1,0:T(8,128)(2,1)S(1)}, u32[]{:S(2)}, u32[]{:S(2)}) %collective-permute-start.46) | collective-permute-done | bytes 147488 | tf_op jit(solution)/shard_map/ppermute | solution.py:765
  255.1 7.4 %token_back.1 = f32[512,768]{1,0:T(8,128)} custom-call(s32[3]{0:T(128)S(1)} %pad_add_fusion.info.refs_7_, bf16[4,64,512]{2,1,0:T(8,128)(2,1)S(1)} %add_convert_fusion.13.l0, bf16[4,64,512]{2,1,0:T(8,128)(2,1)S(1)} %collective-permute-done.45.l1, bf16[4,512,768]{2,1,0:T(8,128)(2,1)S(1)} %get-tuple-element.243.joint, f32[512,768]{1,0:T(8,128)S(1)} %copy-done.35, ...), custom_call_target="tpu_custom_call" | custom-call | flops 2415919104 | bytes 10485760 | tf_op jit(solution)/shard_map/token_back/pallas_call | solution.py:57
  302.3 3.7 %collective-permute-done.58 = bf16[192,768]{1,0:T(8,128)(2,1)S(1)} collective-permute-done((bf16[192,768]{1,0:T(8,128)(2,1)S(1)}, bf16[192,768]{1,0:T(8,128)(2,1)S(1)}, u32[]{:S(2)}, u32[]{:S(2)}) %collective-permute-start.58) | collective-permute-done | bytes 294944 | tf_op jit(solution)/shard_map/ppermute | solution.py:765
  315.7 6.5 %collective-permute-done.61 = bf16[96,768]{1,0:T(8,128)(2,1)S(1)} collective-permute-done((bf16[96,768]{1,0:T(8,128)(2,1)S(1)}, bf16[96,768]{1,0:T(8,128)(2,1)S(1)}, u32[]{:S(2)}, u32[]{:S(2)}) %collective-permute-start.61) | collective-permute-done | bytes 147488 | tf_op jit(solution)/shard_map/ppermute | solution.py:765
  326.9 3.9 %collective-permute-done.64 = bf16[192,768]{1,0:T(8,128)(2,1)S(1)} collective-permute-done((bf16[192,768]{1,0:T(8,128)(2,1)S(1)}, bf16[192,768]{1,0:T(8,128)(2,1)S(1)}, u32[]{:S(2)}, u32[]{:S(2)}) %collective-permute-start.64) | collective-permute-done | bytes 294944 | tf_op jit(solution)/shard_map/ppermute | solution.py:765
  (451 shorter events, 161.7 us)
Async XLA Ops:
  6.1 21.6 %collective-permute-start.5 = (bf16[512,768]{1,0:T(8,128)(2,1)S(1)}, bf16[512,768]{1,0:T(8,128)(2,1)S(1)}, u32[]{:S(2)}, u32[]{:S(2)}) collective-permute-start(bf16[512,768]{1,0:T(8,128)(2,1)S(1)} %bitcast.67), channel_id=1, source_target_pairs={{0,1},{1,0},{2,3},{3,2},{4,5},{5,4},{6,7},{7,6},{8,9},{9,8},{10,11... | collective-permute-start | bytes 2359304 | tf_op jit(solution)/shard_map/ppermute | solution.py:724
  8.7 27.0 %collective-permute-start.10 = (bf16[608,768]{1,0:T(8,128)(2,1)S(1)}, bf16[608,768]{1,0:T(8,128)(2,1)}, u32[]{:S(2)}, u32[]{:S(2)}) collective-permute-start(bf16[608,768]{1,0:T(8,128)(2,1)S(1)} %constant_dynamic-update-slice_fusion.wt.w0), channel_id=1, source_target_pairs={{0,1},{1,0},{2,3},{3,2},{4,5},{5,4},{6,7},{7,6},{8,9},{9,8},{10,11... | collective-permute-start | bytes 2801672 | tf_op jit(solution)/shard_map/ppermute | solution.py:724
  10.5 17.2 %collective-permute-start.4 = (bf16[32,768]{1,0:T(8,128)(2,1)S(1)}, bf16[32,768]{1,0:T(8,128)(2,1)S(1)}, u32[]{:S(2)}, u32[]{:S(2)}) collective-permute-start(bf16[32,768]{1,0:T(8,128)(2,1)S(1)} %select_bitcast_fusion), channel_id=1, source_target_pairs={{1,2},{2,1},{5,6},{6,5},{9,10},{10,9},{13,14},{14,13},{17,18},{18,... | collective-permute-start | bytes 147464 | tf_op jit(solution)/shard_map/ppermute | solution.py:769
  11.2 14.5 %collective-permute-start.3 = (bf16[608,384]{1,0:T(8,128)(2,1)S(1)}, bf16[608,384]{1,0:T(8,128)(2,1)S(1)}, u32[]{:S(2)}, u32[]{:S(2)}) collective-permute-start(bf16[608,384]{1,0:T(8,128)(2,1)S(1)} %constant_dynamic-slice_fusion.16), channel_id=1, source_target_pairs={{0,2},{1,3},{2,0},{3,1},{4,6},{5,7},{6,4},{7,5},{8,10},{9,11},{10,... | collective-permute-start | bytes 1400840 | tf_op jit(solution)/shard_map/ppermute | solution.py:724
  34.6 17.6 %collective-permute-start.16 = (bf16[960,384]{1,0:T(8,128)(2,1)S(1)}, bf16[960,384]{1,0:T(8,128)(2,1)S(1)}, u32[]{:S(2)}, u32[]{:S(2)}) collective-permute-start(bf16[960,384]{1,0:T(8,128)(2,1)S(1)} %constant_dynamic-slice_fusion.15), channel_id=1, source_target_pairs={{0,2},{1,3},{2,0},{3,1},{4,6},{5,7},{6,4},{7,5},{8,10},{9,11},{10,... | collective-permute-start | bytes 2211848 | tf_op jit(solution)/shard_map/ppermute | solution.py:724
  46.2 32.7 %collective-permute-start.18 = (bf16[960,768]{1,0:T(8,128)(2,1)S(1)}, bf16[960,768]{1,0:T(8,128)(2,1)S(1)}, u32[]{:S(2)}, u32[]{:S(2)}) collective-permute-start(bf16[960,768]{1,0:T(8,128)(2,1)S(1)} %constant_dynamic-update-slice_fusion.4), channel_id=1, source_target_pairs={{0,1},{1,0},{2,3},{3,2},{4,5},{5,4},{6,7},{7,6},{8,9},{9,8},{10,11... | collective-permute-start | bytes 4423688 | tf_op jit(solution)/shard_map/ppermute | solution.py:724
  52.3 20.1 %collective-permute-start.17 = (bf16[960,384]{1,0:T(8,128)(2,1)S(1)}, bf16[960,384]{1,0:T(8,128)(2,1)S(1)}, u32[]{:S(2)}, u32[]{:S(2)}) collective-permute-start(bf16[960,384]{1,0:T(8,128)(2,1)S(1)} %collective-permute-done.16.o1.w1.refs_13_), channel_id=1, source_target_pairs={{0,4},{4,0},{8,12},{12,8},{16,20},{20,16},{24,28},{28,24},{1,5},{5... | collective-permute-start | bytes 2211848 | tf_op jit(solution)/shard_map/ppermute | solution.py:765
  62.7 15.1 %collective-permute-start.21 = (bf16[768,384]{1,0:T(8,128)(2,1)S(1)}, bf16[768,384]{1,0:T(8,128)(2,1)S(1)}, u32[]{:S(2)}, u32[]{:S(2)}) collective-permute-start(bf16[768,384]{1,0:T(8,128)(2,1)S(1)} %constant_dynamic-slice_fusion.14), channel_id=1, source_target_pairs={{0,2},{1,3},{2,0},{3,1},{4,6},{5,7},{6,4},{7,5},{8,10},{9,11},{10,... | collective-permute-start | bytes 1769480 | tf_op jit(solution)/shard_map/ppermute | solution.py:724
  77.9 14.2 %collective-permute-start.22 = (bf16[768,384]{1,0:T(8,128)(2,1)S(1)}, bf16[768,384]{1,0:T(8,128)(2,1)S(1)}, u32[]{:S(2)}, u32[]{:S(2)}) collective-permute-start(bf16[768,384]{1,0:T(8,128)(2,1)S(1)} %collective-permute-done.21.w1), channel_id=1, source_target_pairs={{0,4},{4,0},{8,12},{12,8},{16,20},{20,16},{24,28},{28,24},{1,5},{5... | collective-permute-start | bytes 1769480 | tf_op jit(solution)/shard_map/ppermute | solution.py:765
  78.8 22.7 %collective-permute-start.23 = (bf16[768,768]{1,0:T(8,128)(2,1)S(1)}, bf16[768,768]{1,0:T(8,128)(2,1)S(1)}, u32[]{:S(2)}, u32[]{:S(2)}) collective-permute-start(bf16[768,768]{1,0:T(8,128)(2,1)S(1)} %copy-done.30), channel_id=1, source_target_pairs={{0,1},{1,0},{2,3},{3,2},{4,5},{5,4},{6,7},{7,6},{8,9},{9,8},{10,11... | collective-permute-start | bytes 3538952 | tf_op jit(solution)/shard_map/ppermute | solution.py:724
  101.4 17.0 %collective-permute-start.26 = (bf16[3,512,768]{2,1,0:T(8,128)(2,1)}, bf16[3,512,768]{2,1,0:T(8,128)(2,1)}, u32[]{:S(2)}, u32[]{:S(2)}) collective-permute-start(bf16[3,512,768]{2,1,0:T(8,128)(2,1)} %get-tuple-element.172), channel_id=1, source_target_pairs={{0,1},{1,0},{2,3},{3,2},{4,5},{5,4},{6,7},{7,6},{8,9},{9,8},{10,11... | collective-permute-start | bytes 7077896 | tf_op jit(solution)/shard_map/ppermute | solution.py:724
  133.9 17.4 %collective-permute-start.29 = (bf16[384,768]{1,0:T(8,128)(2,1)}, bf16[384,768]{1,0:T(8,128)(2,1)}, u32[]{:S(2)}, u32[]{:S(2)}) collective-permute-start(bf16[384,768]{1,0:T(8,128)(2,1)} %get-tuple-element.182), channel_id=1, source_target_pairs={{0,8},{4,12},{8,0},{12,4},{16,24},{20,28},{24,16},{28,20},{1,9},{5... | collective-permute-start | bytes 1769480 | tf_op jit(solution)/shard_map/ppermute | solution.py:765
  134.6 16.7 %collective-permute-start.28 = (bf16[384,768]{1,0:T(8,128)(2,1)}, bf16[384,768]{1,0:T(8,128)(2,1)}, u32[]{:S(2)}, u32[]{:S(2)}) collective-permute-start(bf16[384,768]{1,0:T(8,128)(2,1)} %get-tuple-element.177), channel_id=1, source_target_pairs={{0,4},{4,0},{8,12},{12,8},{16,20},{20,16},{24,28},{28,24},{1,5},{5... | collective-permute-start | bytes 1769480 | tf_op jit(solution)/shard_map/ppermute | solution.py:765
  152.1 14.8 %collective-permute-start.33 = (bf16[384,768]{1,0:T(8,128)(2,1)S(1)}, bf16[384,768]{1,0:T(8,128)(2,1)S(1)}, u32[]{:S(2)}, u32[]{:S(2)}) collective-permute-start(bf16[384,768]{1,0:T(8,128)(2,1)S(1)} %copy-done.72), channel_id=1, source_target_pairs={{0,8},{4,12},{8,0},{12,4},{16,24},{20,28},{24,16},{28,20},{1,9},{5... | collective-permute-start | bytes 1769480 | tf_op jit(solution)/shard_map/ppermute | solution.py:765
  152.6 14.3 %collective-permute-start.32 = (bf16[384,768]{1,0:T(8,128)(2,1)S(1)}, bf16[384,768]{1,0:T(8,128)(2,1)S(1)}, u32[]{:S(2)}, u32[]{:S(2)}) collective-permute-start(bf16[384,768]{1,0:T(8,128)(2,1)S(1)} %copy-done.70), channel_id=1, source_target_pairs={{0,4},{4,0},{8,12},{12,8},{16,20},{20,16},{24,28},{28,24},{1,5},{5... | collective-permute-start | bytes 1769480 | tf_op jit(solution)/shard_map/ppermute | solution.py:765
  170.2 15.3 %collective-permute-start.36 = (bf16[2,192,768]{2,1,0:T(8,128)(2,1)S(1)}, bf16[2,192,768]{2,1,0:T(8,128)(2,1)S(1)}, u32[]{:S(2)}, u32[]{:S(2)}) collective-permute-start(bf16[2,192,768]{2,1,0:T(8,128)(2,1)S(1)} %pad_maximum_fusion.1), channel_id=1, source_target_pairs={{0,8},{4,12},{8,0},{12,4},{16,24},{20,28},{24,16},{28,20},{1,9},{5... | collective-permute-start | bytes 1769480 | tf_op jit(solution)/shard_map/ppermute | solution.py:765
  172.0 15.0 %collective-permute-start.37 = (bf16[2,192,768]{2,1,0:T(8,128)(2,1)S(1)}, bf16[2,192,768]{2,1,0:T(8,128)(2,1)S(1)}, u32[]{:S(2)}, u32[]{:S(2)}) collective-permute-start(bf16[2,192,768]{2,1,0:T(8,128)(2,1)S(1)} %pad_maximum_fusion.2), channel_id=1, source_target_pairs={{0,4},{4,0},{8,12},{12,8},{16,20},{20,16},{24,28},{28,24},{1,5},{5... | collective-permute-start | bytes 1769480 | tf_op jit(solution)/shard_map/ppermute | solution.py:765
  209.4 24.7 %collective-permute-start.41 = (bf16[384,768]{1,0:T(8,128)(2,1)}, bf16[384,768]{1,0:T(8,128)(2,1)}, u32[]{:S(2)}, u32[]{:S(2)}) collective-permute-start(bf16[384,768]{1,0:T(8,128)(2,1)} %get-tuple-element.229), channel_id=1, source_target_pairs={{0,2},{1,3},{2,0},{3,1},{4,6},{5,7},{6,4},{7,5},{8,10},{9,11},{10,... | collective-permute-start | bytes 1769480 | tf_op jit(solution)/shard_map/ppermute | solution.py:724
  212.9 21.2 %collective-permute-start.42 = (bf16[96,768]{1,0:T(8,128)(2,1)}, bf16[96,768]{1,0:T(8,128)(2,1)}, u32[]{:S(2)}, u32[]{:S(2)}) collective-permute-start(bf16[96,768]{1,0:T(8,128)(2,1)} %get-tuple-element.338), channel_id=1, source_target_pairs={{0,16},{4,20},{8,24},{12,28},{16,0},{20,4},{24,8},{28,12},{1,17},{... | collective-permute-start | bytes 442376 | tf_op jit(solution)/shard_map/ppermute | solution.py:765
  217.2 16.9 %collective-permute-start.43 = (bf16[96,768]{1,0:T(8,128)(2,1)}, bf16[96,768]{1,0:T(8,128)(2,1)}, u32[]{:S(2)}, u32[]{:S(2)}) collective-permute-start(bf16[96,768]{1,0:T(8,128)(2,1)} %get-tuple-element.336), channel_id=1, source_target_pairs={{0,16},{4,20},{8,24},{12,28},{16,0},{20,4},{24,8},{28,12},{1,17},{... | collective-permute-start | bytes 442376 | tf_op jit(solution)/shard_map/ppermute | solution.py:765
  236.2 13.7 %collective-permute-start.46 = (bf16[96,768]{1,0:T(8,128)(2,1)S(1)}, bf16[96,768]{1,0:T(8,128)(2,1)S(1)}, u32[]{:S(2)}, u32[]{:S(2)}) collective-permute-start(bf16[96,768]{1,0:T(8,128)(2,1)S(1)} %add_convert_fusion.17), channel_id=1, source_target_pairs={{0,16},{4,20},{8,24},{12,28},{16,0},{20,4},{24,8},{28,12},{1,17},{... | collective-permute-start | bytes 442376 | tf_op jit(solution)/shard_map/ppermute | solution.py:765
  239.0 14.7 %collective-permute-start.45 = (bf16[4,64,512]{2,1,0:T(8,128)(2,1)S(1)}, bf16[4,64,512]{2,1,0:T(8,128)(2,1)S(1)}, u32[]{:S(2)}, u32[]{:S(2)}) collective-permute-start(bf16[4,64,512]{2,1,0:T(8,128)(2,1)S(1)} %add_convert_fusion.13.l0), channel_id=1, source_target_pairs={{0,2},{1,3},{2,0},{3,1},{4,6},{5,7},{6,4},{7,5},{8,10},{9,11},{10,... | collective-permute-start | bytes 786440 | tf_op jit(solution)/shard_map/ppermute | solution.py:724
  254.2 15.3 %collective-permute-start.48 = (bf16[384,768]{1,0:T(8,128)(2,1)S(1)}, bf16[384,768]{1,0:T(8,128)(2,1)S(1)}, u32[]{:S(2)}, u32[]{:S(2)}) collective-permute-start(bf16[384,768]{1,0:T(8,128)(2,1)S(1)} %copy-done.68), channel_id=1, source_target_pairs={{0,2},{1,3},{2,0},{3,1},{4,6},{5,7},{6,4},{7,5},{8,10},{9,11},{10,... | collective-permute-start | bytes 1769480 | tf_op jit(solution)/shard_map/ppermute | solution.py:724
  309.6 14.1 %collective-permute-start.71 = (bf16[192,768]{1,0:T(8,128)(2,1)S(1)}, bf16[192,768]{1,0:T(8,128)(2,1)S(1)}, u32[]{:S(2)}, u32[]{:S(2)}) collective-permute-start(bf16[192,768]{1,0:T(8,128)(2,1)S(1)} %slice.235), channel_id=1, source_target_pairs={{0,4},{4,0},{8,12},{12,8},{16,20},{20,16},{24,28},{28,24},{1,5},{5... | collective-permute-start | bytes 884744 | tf_op jit(solution)/shard_map/ppermute | solution.py:765
  (140 other events, 1262.9 us)
where the time goes:
time: 334 us; the launch traced here: 333 us
  waiting for transfers between devices  108 us (32%)
  Pallas kernels  108 us (32%)
  starting transfers between devices  64.8 us (19%)
  local copies, waits for them, and re-layouts  31.6 us (9%)
  other arithmetic  16.1 us (5%)
    pallas_call x14, Pallas kernels, call(): pl.pallas_call(body, out_shape=[jax.ShapeDtypeStruct(s, d) for s, d in ou...  103 us
    ppermute x34, waiting for transfers between devices, hop_batch(): return lax.ppermute(x, 'batch', [(i, i ^ step) for i in range(batch_count)])  65.1 us
    ppermute x36, waiting for transfers between devices, hop(): return lax.ppermute(x, 'head', [(i, i ^ HOP[step]) for i in range(4)])  42.4 us
    ppermute x34, starting transfers between devices, hop_batch(): return lax.ppermute(x, 'batch', [(i, i ^ step) for i in range(batch_count)])  39.7 us
    ppermute x36, starting transfers between devices, hop(): return lax.ppermute(x, 'head', [(i, i ^ HOP[step]) for i in range(4)])  23.7 us
    unnamed x190, local copies, waits for them, and re-layouts  20.9 us
    convert_element_type x18, other arithmetic, add_all(): (a.astype(f32) + b.astype(f32)).astype(bf16)  6.94 us
  transfers between devices with their start and end apart: 72, of which 32 were waited for; matrix products, arithmetic and copies ran while one was open for 8% of the time, Pallas kernels for 30%

commit v1 on v0

--- a/solution.py
+++ b/solution.py
@@ -15,7 +15,7 @@
 TAPS = 65
 HALO = TAPS // 2
 EARLY = 1
-LATE = 0
+LATE = 2
 IDLE = 1
 GROUP = 256
 NN = ((1,), (0,))
@@ -1055,7 +1055,7 @@
     if EARLY >= 1:
         d_down, d_up = after((d_down, d_up), partial)
         d_down, d_up = down_rest[0](d_down), up_rest[0](d_up)
-        partial, partial_across = after((partial, partial_across), partial_across, d_down[0], d_up[0])
+        partial, partial_across = after((partial, partial_across), partial_across)
         down_rest, up_rest = down_rest[1:], up_rest[1:]
     else:
         partial, partial_across = after((partial, partial_across), partial_across)

time: 334 us -> 331 us (level)
    unnamed x190 -> x188, local copies, waits for them, and re-layouts: 20.9 us -> 21.3 us
  transfers between devices with their start and end apart: 72 -> 72, of which waited for: 32 -> 34; matrix products, arithmetic and copies ran while one was open for 8% -> 8% of each run, Pallas kernels for 30% -> 30%
where the time goes in v1:
time: 331 us; the launch traced here: 330 us
  Pallas kernels  108 us (33%)
  waiting for transfers between devices  105 us (32%)
  starting transfers between devices  65.7 us (20%)
  local copies, waits for them, and re-layouts  32 us (10%)
  other arithmetic  14.1 us (4%)
    pallas_call x14, Pallas kernels, call(): pl.pallas_call(body, out_shape=[jax.ShapeDtypeStruct(s, d) for s, d in ou...  103 us
    ppermute x34, waiting for transfers between devices, hop_batch(): return lax.ppermute(x, 'batch', [(i, i ^ step) for i in range(batch_count)])  65 us
    ppermute x34, starting transfers between devices, hop_batch(): return lax.ppermute(x, 'batch', [(i, i ^ step) for i in range(batch_count)])  40.7 us
    ppermute x36, waiting for transfers between devices, hop(): return lax.ppermute(x, 'head', [(i, i ^ HOP[step]) for i in range(4)])  40.3 us
    ppermute x36, starting transfers between devices, hop(): return lax.ppermute(x, 'head', [(i, i ^ HOP[step]) for i in range(4)])  23.7 us
    unnamed x188, local copies, waits for them, and re-layouts  21.3 us
    convert_element_type x18, other arithmetic, add_all(): (a.astype(f32) + b.astype(f32)).astype(bf16)  6.98 us
  transfers between devices with their start and end apart: 72, of which 34 were waited for; matrix products, arithmetic and copies ran while one was open for 8% of the time, Pallas kernels for 30%

profile of v1, /device:TPU:0, one launch (start us, length us, event | category | flops | bytes accessed | tf_op | source)
XLA Modules:
  0.0 330.4 jit_solution(9780220098216412077)
XLA Ops:
  11.2 3.3 %collective-permute-start.3 = (bf16[608,384]{1,0:T(8,128)(2,1)S(1)}, bf16[608,384]{1,0:T(8,128)(2,1)S(1)}, u32[]{:S(2)}, u32[]{:S(2)}) collective-permute-start(bf16[608,384]{1,0:T(8,128)(2,1)S(1)} %constant_dynamic-slice_fusion.16), channel_id=1, source_target_pairs={{0,2},{1,3},{2,0},{3,1},{4,6},{5,7},{6,4},{7,5},{8,10},{9,11},{10,... | collective-permute-start | bytes 1400840 | tf_op jit(solution)/shard_map/ppermute | solution.py:724
  14.8 8.7 %landmarks.1 = (f32[64,768]{1,0:T(8,128)S(1)}, bf16[64,768]{1,0:T(8,128)(2,1)S(1)}, f32[6,4,3,64,64]{4,3,2,1,0:T(8,128)S(1)}) custom-call(bf16[64,768]{1,0:T(8,128)(2,1)S(1)} %fusion.1.p0, bf16[64,768]{1,0:T(8,128)(2,1)S(1)} %collective-permute-done.p1, bf16[64,768]{1,0:T(8,128)(2,1)S(1)} %collective-permute-done.1.p2, ...), custom_call_target="tpu_custom_call" | custom-call | flops 1000000000 | bytes 4194304 | tf_op jit(solution)/shard_map/landmarks/pallas_call | solution.py:57
  30.1 4.5 %collective-permute-done.6 = f32[64,768]{1,0:T(8,128)S(1)} collective-permute-done((f32[64,768]{1,0:T(8,128)S(1)}, f32[64,768]{1,0:T(8,128)S(1)}, u32[]{:S(2)}, u32[]{:S(2)}) %collective-permute-start.6) | collective-permute-done | bytes 196640 | tf_op jit(solution)/shard_map/ppermute | solution.py:724
  40.7 5.4 %project.1 = (bf16[4,512,256]{2,1,0:T(8,128)(2,1)S(1)}, bf16[4,512,256]{2,1,0:T(8,128)(2,1)S(1)}, bf16[4,640,256]{2,1,0:T(8,128)(2,1)S(1)}) custom-call(s32[3]{0:T(128)S(1)} %pad_add_fusion.info.refs_7_, bf16[512,768]{1,0:T(8,128)(2,1)S(1)} %bitcast.68, bf16[32,768]{1,0:T(8,128)(2,1)S(1)} %get-tuple-element.310.before, ...), custom_call_target="tpu_custom_call" | custom-call | flops 2415919104 | bytes 8388608 | tf_op jit(solution)/shard_map/project/pallas_call | solution.py:57
  46.4 5.9 %collective-permute-done.16.o1.w1.refs_13_ = bf16[960,384]{1,0:T(8,128)(2,1)S(1)} collective-permute-done((bf16[960,384]{1,0:T(8,128)(2,1)S(1)}, bf16[960,384]{1,0:T(8,128)(2,1)S(1)}, u32[]{:S(2)}, u32[]{:S(2)}) %collective-permute-start.16) | collective-permute-done | bytes 737312 | tf_op jit(solution)/shard_map/ppermute | solution.py:724
  52.6 4.2 %third.1.p0 = bf16[4,64,256]{2,1,0:T(8,128)(2,1)S(1)} custom-call(s32[3]{0:T(128)S(1)} %pad_add_fusion.info.refs_7_, f32[4,64,768]{2,1,0:T(8,128)S(1)} %pad_maximum_fusion.lm, bf16[4,512,256]{2,1,0:T(8,128)(2,1)S(1)} %get-tuple-element.155.k_ref, bf16[4,640,256]{2,1,0:T(8,128)(2,1)S(1)} %get-tuple-element.156.v_ref), custom_call_target="tpu_custom_call" | custom-call | flops 1000000000 | bytes 3145728 | tf_op jit(solution)/shard_map/third/pallas_call | solution.py:57
  59.1 3.6 %collective-permute-done.15.p3 = bf16[4,64,256]{2,1,0:T(8,128)(2,1)S(1)} collective-permute-done((bf16[4,64,256]{2,1,0:T(8,128)(2,1)S(1)}, bf16[4,64,256]{2,1,0:T(8,128)(2,1)S(1)}, u32[]{:S(2)}, u32[]{:S(2)}) %collective-permute-start.15) | collective-permute-done | bytes 131104 | tf_op jit(solution)/shard_map/ppermute | solution.py:724
  64.9 6.7 %context.1 = (bf16[4,512,256]{2,1,0:T(8,128)(2,1)S(1)}, f32[4,64,256]{2,1,0:T(8,128)S(1)}, f32[4,64,256]{2,1,0:T(8,128)S(1)}) custom-call(bf16[4,64,256]{2,1,0:T(8,128)(2,1)S(1)} %third.1.p0, bf16[4,64,256]{2,1,0:T(8,128)(2,1)S(1)} %collective-permute-done.13.p1, bf16[4,64,256]{2,1,0:T(8,128)(2,1)S(1)} %collective-permute-done.14.p2, ...), custom_call_target="tpu_custom_call" | custom-call | flops 3000000000 | bytes 5242880 | tf_op jit(solution)/shard_map/context/pallas_call | solution.py:57
  73.0 4.9 %collective-permute-done.21.w1 = bf16[768,384]{1,0:T(8,128)(2,1)S(1)} collective-permute-done((bf16[768,384]{1,0:T(8,128)(2,1)S(1)}, bf16[768,384]{1,0:T(8,128)(2,1)S(1)}, u32[]{:S(2)}, u32[]{:S(2)}) %collective-permute-start.21) | collective-permute-done | bytes 589856 | tf_op jit(solution)/shard_map/ppermute | solution.py:724
  83.0 9.0 %collective-permute-done.22.w2 = bf16[768,384]{1,0:T(8,128)(2,1)S(1)} collective-permute-done((bf16[768,384]{1,0:T(8,128)(2,1)S(1)}, bf16[768,384]{1,0:T(8,128)(2,1)S(1)}, u32[]{:S(2)}, u32[]{:S(2)}) %collective-permute-start.22) | collective-permute-done | bytes 589856 | tf_op jit(solution)/shard_map/ppermute | solution.py:765
  92.7 8.7 %up.1 = (bf16[4,512,768]{2,1,0:T(8,128)(2,1)S(1)}, bf16[4,512,768]{2,1,0:T(8,128)(2,1)}, bf16[3,512,768]{2,1,0:T(8,128)(2,1)}) custom-call(s32[3]{0:T(128)S(1)} %pad_add_fusion.info.refs_7_, bf16[512,768]{1,0:T(8,128)(2,1)S(1)} %get-tuple-element.165.low.refs_6_, f32[4,8,768]{2,1,0:T(8,128)S(1)} %pad_maximum_fusion.11.small, ...), custom_call_target="tpu_custom_call" | custom-call | flops 2415919104 | bytes 12582912 | tf_op jit(solution)/shard_map/up/pallas_call | solution.py:57
  101.6 6.5 %down.1 = (bf16[512,768]{1,0:T(8,128)(2,1)}, f32[512,768]{1,0:T(8,128)S(1)}, bf16[512,768]{1,0:T(8,128)(2,1)S(1)}, f32[8,768]{1,0:T(8,128)S(1)}) custom-call(s32[3]{0:T(128)S(1)} %pad_add_fusion.info.refs_7_, bf16[4,512,768]{2,1,0:T(8,128)(2,1)S(1)} %get-tuple-element.166.hidden.refs_1_, f32[512,768]{1,0:T(8,128)S(1)} %get-tuple-element.167.normed, ...), custom_call_target="tpu_custom_call" | custom-call | flops 2415919104 | bytes 14680064 | tf_op jit(solution)/shard_map/down/pallas_call | solution.py:57
  109.2 6.4 %hidden_back.1 = (bf16[4,512,768]{2,1,0:T(8,128)(2,1)S(1)}, bf16[3,512,768]{2,1,0:T(8,128)(2,1)}, f32[4,8,768]{2,1,0:T(8,128)S(1)}) custom-call(s32[3]{0:T(128)S(1)} %pad_add_fusion.info.refs_7_, bf16[512,768]{1,0:T(8,128)(2,1)S(1)} %get-tuple-element.180.dlow.refs_3_, bf16[4,512,768]{2,1,0:T(8,128)(2,1)S(1)} %copy-done.73, bf16[768,768]{1,0:T(8,128)(2,1)S(1)} %copy-done.30, ...), custom_call_target="tpu_custom_call" | custom-call | flops 2415919104 | bytes 12582912 | tf_op jit(solution)/shard_map/hidden_back/pallas_call | solution.py:57
  118.5 4.4 %collective-permute-done.27.refs_4_ = bf16[3,512,768]{2,1,0:T(8,128)(2,1)} collective-permute-done((bf16[3,512,768]{2,1,0:T(8,128)(2,1)}, bf16[3,512,768]{2,1,0:T(8,128)(2,1)}, u32[]{:S(2)}, u32[]{:S(2)}) %collective-permute-start.27) | collective-permute-done | bytes 2359328 | tf_op jit(solution)/shard_map/ppermute | solution.py:724
  125.2 7.1 %grad_sent.1 = (bf16[384,768]{1,0:T(8,128)(2,1)}, bf16[384,768]{1,0:T(8,128)(2,1)S(1)}, bf16[384,768]{1,0:T(8,128)(2,1)}, bf16[384,768]{1,0:T(8,128)(2,1)S(1)}) custom-call(s32[2]{0:T(128)S(1)} %get-tuple-element.291.refs_0_, bf16[4,512,768]{2,1,0:T(8,128)(2,1)} %copy-done.1, bf16[3,512,768]{2,1,0:T(8,128)(2,1)} %collective-permute-done.26.refs_2_, ...), custom_call_target="tpu_custom_call" | custom-call | flops 5000000000 | bytes 10485760 | tf_op jit(solution)/shard_map/grad_sent/pallas_call | solution.py:57
  136.1 15.2 %grad_kept.1 = (bf16[384,768]{1,0:T(8,128)(2,1)S(1)}, bf16[384,768]{1,0:T(8,128)(2,1)S(1)}, bf16[384,768]{1,0:T(8,128)(2,1)S(1)}, bf16[384,768]{1,0:T(8,128)(2,1...) custom-call(s32[2]{0:T(128)S(1)} %get-tuple-element.292.refs_0_, ...), custom_call_target="tpu_custom_call" | custom-call | flops 5000000000 | bytes 10485760 | tf_op jit(solution)/shard_map/grad_kept/pallas_call | solution.py:57
  157.6 9.4 %first_back.1 = (f32[4,64,256]{2,1,0:T(8,128)S(1)}, bf16[4,512,256]{2,1,0:T(8,128)(2,1)S(1)}, f32[4,64,256]{2,1,0:T(8,128)S(1)}, f32[4,512,256]{2,1,0:T(8,128)S(1)}, f32[4,8,256]{2,1,0:T(8,128)S(1)}) custom-call(s32[3]{0:T(128)S(1)} %pad_add_fusion.info.refs_7_, bf16[512,768]{1,0:T(8,128)(2,1)S(1)} %get-tuple-element.244.g_ref.g, ...), custom_call_target="tpu_custom_call" | custom-call | flops 5000000000 | bytes 10485760 | tf_op jit(solution)/shard_map/first_back/pallas_call | solution.py:57
  174.1 11.3 %collective-permute-done.36 = bf16[2,192,768]{2,1,0:T(8,128)(2,1)S(1)} collective-permute-done((bf16[2,192,768]{2,1,0:T(8,128)(2,1)S(1)}, bf16[2,192,768]{2,1,0:T(8,128)(2,1)S(1)}, u32[]{:S(2)}, u32[]{:S(2)}) %collective-permute-start.36) | collective-permute-done | bytes 589856 | tf_op jit(solution)/shard_map/ppermute | solution.py:765
  189.6 4.9 %third_back.1 = (bf16[4,512,768]{2,1,0:T(8,128)(2,1)S(1)}, bf16[2,512,1024]{2,1,0:T(8,128)(2,1)S(1)}, f32[4,64,512]{2,1,0:T(8,128)S(1)}) custom-call(s32[3]{0:T(128)S(1)} %pad_add_fusion.info.refs_7_, f32[4,64,256]{2,1,0:T(8,128)S(1)} %maximum_add_fusion.1.x0, f32[4,64,256]{2,1,0:T(8,128)S(1)} %collective-permute-done.35.x1, f32[4,64,768]{2,1,0:T(8,128)S(1)} %copy-done.44, ...), custom_call_target="tpu_custom_call" | custom-call | flops 5000000000 | bytes 8388608 | tf_op jit(solution)/shard_map/third_back/pallas_call | solution.py:57
  197.4 4.2 %collective-permute-done.38 = bf16[192,768]{1,0:T(8,128)(2,1)S(1)} collective-permute-done((bf16[192,768]{1,0:T(8,128)(2,1)S(1)}, bf16[192,768]{1,0:T(8,128)(2,1)S(1)}, u32[]{:S(2)}, u32[]{:S(2)}) %collective-permute-start.38) | collective-permute-done | bytes 294944 | tf_op jit(solution)/shard_map/ppermute | solution.py:724
  224.7 9.4 %inverse_back.1 = bf16[4,64,512]{2,1,0:T(8,128)(2,1)S(1)} custom-call(f32[4,64,256]{2,1,0:T(8,128)S(1)} %maximum_add_fusion.1.x0, f32[4,64,256]{2,1,0:T(8,128)S(1)} %copy-done.60, f32[4,64,256]{2,1,0:T(8,128)S(1)} %copy-done.58, f32[64,768]{1,0:T(8,128)S(1)} %copy-done.42, f32[6,4,3,64,64]{4,3,2,1,0:T(8,128)S(1)} %copy-done.32, f32[4,64,512]{2,1,0:T(8,128)S(1)} %copy-done.47), custom_call_target="tpu_custom_call" | custom-call | flops 1000000000 | bytes 4194304 | tf_op jit(solution)/shard_map/inverse_back/pallas_call | solution.py:57
  239.7 10.2 %collective-permute-done.53 = bf16[96,768]{1,0:T(8,128)(2,1)S(1)} collective-permute-done((bf16[96,768]{1,0:T(8,128)(2,1)S(1)}, bf16[96,768]{1,0:T(8,128)(2,1)S(1)}, u32[]{:S(2)}, u32[]{:S(2)}) %collective-permute-start.53) | collective-permute-done | bytes 147488 | tf_op jit(solution)/shard_map/ppermute | solution.py:765
  254.9 7.4 %token_back.1 = f32[512,768]{1,0:T(8,128)} custom-call(s32[3]{0:T(128)S(1)} %pad_add_fusion.info.refs_7_, bf16[4,64,512]{2,1,0:T(8,128)(2,1)S(1)} %add_convert_fusion.13.l0, bf16[4,64,512]{2,1,0:T(8,128)(2,1)S(1)} %collective-permute-done.45.l1, bf16[4,512,768]{2,1,0:T(8,128)(2,1)S(1)} %get-tuple-element.239.joint, f32[512,768]{1,0:T(8,128)S(1)} %copy-done.35, ...), custom_call_target="tpu_custom_call" | custom-call | flops 2415919104 | bytes 10485760 | tf_op jit(solution)/shard_map/token_back/pallas_call | solution.py:57
  274.0 4.9 %collective-permute-done.48 = bf16[192,768]{1,0:T(8,128)(2,1)S(1)} collective-permute-done((bf16[192,768]{1,0:T(8,128)(2,1)S(1)}, bf16[192,768]{1,0:T(8,128)(2,1)S(1)}, u32[]{:S(2)}, u32[]{:S(2)}) %collective-permute-start.48) | collective-permute-done | bytes 294944 | tf_op jit(solution)/shard_map/ppermute | solution.py:765
  (449 shorter events, 161.0 us)
Async XLA Ops:
  6.1 21.6 %collective-permute-start.5 = (bf16[512,768]{1,0:T(8,128)(2,1)S(1)}, bf16[512,768]{1,0:T(8,128)(2,1)S(1)}, u32[]{:S(2)}, u32[]{:S(2)}) collective-permute-start(bf16[512,768]{1,0:T(8,128)(2,1)S(1)} %bitcast.67), channel_id=1, source_target_pairs={{0,1},{1,0},{2,3},{3,2},{4,5},{5,4},{6,7},{7,6},{8,9},{9,8},{10,11... | collective-permute-start | bytes 2359304 | tf_op jit(solution)/shard_map/ppermute | solution.py:724
  8.7 27.0 %collective-permute-start.10 = (bf16[608,768]{1,0:T(8,128)(2,1)S(1)}, bf16[608,768]{1,0:T(8,128)(2,1)}, u32[]{:S(2)}, u32[]{:S(2)}) collective-permute-start(bf16[608,768]{1,0:T(8,128)(2,1)S(1)} %constant_dynamic-update-slice_fusion.wt.w0), channel_id=1, source_target_pairs={{0,1},{1,0},{2,3},{3,2},{4,5},{5,4},{6,7},{7,6},{8,9},{9,8},{10,11... | collective-permute-start | bytes 2801672 | tf_op jit(solution)/shard_map/ppermute | solution.py:724
  10.5 17.2 %collective-permute-start.4 = (bf16[32,768]{1,0:T(8,128)(2,1)S(1)}, bf16[32,768]{1,0:T(8,128)(2,1)S(1)}, u32[]{:S(2)}, u32[]{:S(2)}) collective-permute-start(bf16[32,768]{1,0:T(8,128)(2,1)S(1)} %select_bitcast_fusion), channel_id=1, source_target_pairs={{1,2},{2,1},{5,6},{6,5},{9,10},{10,9},{13,14},{14,13},{17,18},{18,... | collective-permute-start | bytes 147464 | tf_op jit(solution)/shard_map/ppermute | solution.py:769
  11.2 14.5 %collective-permute-start.3 = (bf16[608,384]{1,0:T(8,128)(2,1)S(1)}, bf16[608,384]{1,0:T(8,128)(2,1)S(1)}, u32[]{:S(2)}, u32[]{:S(2)}) collective-permute-start(bf16[608,384]{1,0:T(8,128)(2,1)S(1)} %constant_dynamic-slice_fusion.16), channel_id=1, source_target_pairs={{0,2},{1,3},{2,0},{3,1},{4,6},{5,7},{6,4},{7,5},{8,10},{9,11},{10,... | collective-permute-start | bytes 1400840 | tf_op jit(solution)/shard_map/ppermute | solution.py:724
  34.6 17.6 %collective-permute-start.16 = (bf16[960,384]{1,0:T(8,128)(2,1)S(1)}, bf16[960,384]{1,0:T(8,128)(2,1)S(1)}, u32[]{:S(2)}, u32[]{:S(2)}) collective-permute-start(bf16[960,384]{1,0:T(8,128)(2,1)S(1)} %constant_dynamic-slice_fusion.15), channel_id=1, source_target_pairs={{0,2},{1,3},{2,0},{3,1},{4,6},{5,7},{6,4},{7,5},{8,10},{9,11},{10,... | collective-permute-start | bytes 2211848 | tf_op jit(solution)/shard_map/ppermute | solution.py:724
  46.2 32.7 %collective-permute-start.18 = (bf16[960,768]{1,0:T(8,128)(2,1)S(1)}, bf16[960,768]{1,0:T(8,128)(2,1)S(1)}, u32[]{:S(2)}, u32[]{:S(2)}) collective-permute-start(bf16[960,768]{1,0:T(8,128)(2,1)S(1)} %constant_dynamic-update-slice_fusion.4), channel_id=1, source_target_pairs={{0,1},{1,0},{2,3},{3,2},{4,5},{5,4},{6,7},{7,6},{8,9},{9,8},{10,11... | collective-permute-start | bytes 4423688 | tf_op jit(solution)/shard_map/ppermute | solution.py:724
  52.3 20.1 %collective-permute-start.17 = (bf16[960,384]{1,0:T(8,128)(2,1)S(1)}, bf16[960,384]{1,0:T(8,128)(2,1)S(1)}, u32[]{:S(2)}, u32[]{:S(2)}) collective-permute-start(bf16[960,384]{1,0:T(8,128)(2,1)S(1)} %collective-permute-done.16.o1.w1.refs_13_), channel_id=1, source_target_pairs={{0,4},{4,0},{8,12},{12,8},{16,20},{20,16},{24,28},{28,24},{1,5},{5... | collective-permute-start | bytes 2211848 | tf_op jit(solution)/shard_map/ppermute | solution.py:765
  62.7 15.1 %collective-permute-start.21 = (bf16[768,384]{1,0:T(8,128)(2,1)S(1)}, bf16[768,384]{1,0:T(8,128)(2,1)S(1)}, u32[]{:S(2)}, u32[]{:S(2)}) collective-permute-start(bf16[768,384]{1,0:T(8,128)(2,1)S(1)} %constant_dynamic-slice_fusion.14), channel_id=1, source_target_pairs={{0,2},{1,3},{2,0},{3,1},{4,6},{5,7},{6,4},{7,5},{8,10},{9,11},{10,... | collective-permute-start | bytes 1769480 | tf_op jit(solution)/shard_map/ppermute | solution.py:724
  77.9 14.2 %collective-permute-start.22 = (bf16[768,384]{1,0:T(8,128)(2,1)S(1)}, bf16[768,384]{1,0:T(8,128)(2,1)S(1)}, u32[]{:S(2)}, u32[]{:S(2)}) collective-permute-start(bf16[768,384]{1,0:T(8,128)(2,1)S(1)} %collective-permute-done.21.w1), channel_id=1, source_target_pairs={{0,4},{4,0},{8,12},{12,8},{16,20},{20,16},{24,28},{28,24},{1,5},{5... | collective-permute-start | bytes 1769480 | tf_op jit(solution)/shard_map/ppermute | solution.py:765
  78.8 22.7 %collective-permute-start.23 = (bf16[768,768]{1,0:T(8,128)(2,1)S(1)}, bf16[768,768]{1,0:T(8,128)(2,1)S(1)}, u32[]{:S(2)}, u32[]{:S(2)}) collective-permute-start(bf16[768,768]{1,0:T(8,128)(2,1)S(1)} %copy-done.30), channel_id=1, source_target_pairs={{0,1},{1,0},{2,3},{3,2},{4,5},{5,4},{6,7},{7,6},{8,9},{9,8},{10,11... | collective-permute-start | bytes 3538952 | tf_op jit(solution)/shard_map/ppermute | solution.py:724
  101.4 17.1 %collective-permute-start.26 = (bf16[3,512,768]{2,1,0:T(8,128)(2,1)}, bf16[3,512,768]{2,1,0:T(8,128)(2,1)}, u32[]{:S(2)}, u32[]{:S(2)}) collective-permute-start(bf16[3,512,768]{2,1,0:T(8,128)(2,1)} %get-tuple-element.174), channel_id=1, source_target_pairs={{0,1},{1,0},{2,3},{3,2},{4,5},{5,4},{6,7},{7,6},{8,9},{9,8},{10,11... | collective-permute-start | bytes 7077896 | tf_op jit(solution)/shard_map/ppermute | solution.py:724
  133.9 17.4 %collective-permute-start.29 = (bf16[384,768]{1,0:T(8,128)(2,1)}, bf16[384,768]{1,0:T(8,128)(2,1)}, u32[]{:S(2)}, u32[]{:S(2)}) collective-permute-start(bf16[384,768]{1,0:T(8,128)(2,1)} %get-tuple-element.184), channel_id=1, source_target_pairs={{0,8},{4,12},{8,0},{12,4},{16,24},{20,28},{24,16},{28,20},{1,9},{5... | collective-permute-start | bytes 1769480 | tf_op jit(solution)/shard_map/ppermute | solution.py:765
  134.6 16.7 %collective-permute-start.28 = (bf16[384,768]{1,0:T(8,128)(2,1)}, bf16[384,768]{1,0:T(8,128)(2,1)}, u32[]{:S(2)}, u32[]{:S(2)}) collective-permute-start(bf16[384,768]{1,0:T(8,128)(2,1)} %get-tuple-element.179), channel_id=1, source_target_pairs={{0,4},{4,0},{8,12},{12,8},{16,20},{20,16},{24,28},{28,24},{1,5},{5... | collective-permute-start | bytes 1769480 | tf_op jit(solution)/shard_map/ppermute | solution.py:765
  152.1 14.8 %collective-permute-start.33 = (bf16[384,768]{1,0:T(8,128)(2,1)S(1)}, bf16[384,768]{1,0:T(8,128)(2,1)S(1)}, u32[]{:S(2)}, u32[]{:S(2)}) collective-permute-start(bf16[384,768]{1,0:T(8,128)(2,1)S(1)} %copy-done.72), channel_id=1, source_target_pairs={{0,8},{4,12},{8,0},{12,4},{16,24},{20,28},{24,16},{28,20},{1,9},{5... | collective-permute-start | bytes 1769480 | tf_op jit(solution)/shard_map/ppermute | solution.py:765
  152.6 14.4 %collective-permute-start.32 = (bf16[384,768]{1,0:T(8,128)(2,1)S(1)}, bf16[384,768]{1,0:T(8,128)(2,1)S(1)}, u32[]{:S(2)}, u32[]{:S(2)}) collective-permute-start(bf16[384,768]{1,0:T(8,128)(2,1)S(1)} %copy-done.70), channel_id=1, source_target_pairs={{0,4},{4,0},{8,12},{12,8},{16,20},{20,16},{24,28},{28,24},{1,5},{5... | collective-permute-start | bytes 1769480 | tf_op jit(solution)/shard_map/ppermute | solution.py:765
  170.2 15.3 %collective-permute-start.36 = (bf16[2,192,768]{2,1,0:T(8,128)(2,1)S(1)}, bf16[2,192,768]{2,1,0:T(8,128)(2,1)S(1)}, u32[]{:S(2)}, u32[]{:S(2)}) collective-permute-start(bf16[2,192,768]{2,1,0:T(8,128)(2,1)S(1)} %pad_maximum_fusion.1), channel_id=1, source_target_pairs={{0,8},{4,12},{8,0},{12,4},{16,24},{20,28},{24,16},{28,20},{1,9},{5... | collective-permute-start | bytes 1769480 | tf_op jit(solution)/shard_map/ppermute | solution.py:765
  172.0 15.0 %collective-permute-start.37 = (bf16[2,192,768]{2,1,0:T(8,128)(2,1)S(1)}, bf16[2,192,768]{2,1,0:T(8,128)(2,1)S(1)}, u32[]{:S(2)}, u32[]{:S(2)}) collective-permute-start(bf16[2,192,768]{2,1,0:T(8,128)(2,1)S(1)} %pad_maximum_fusion.2), channel_id=1, source_target_pairs={{0,4},{4,0},{8,12},{12,8},{16,20},{20,16},{24,28},{28,24},{1,5},{5... | collective-permute-start | bytes 1769480 | tf_op jit(solution)/shard_map/ppermute | solution.py:765
  209.4 24.7 %collective-permute-start.41 = (bf16[384,768]{1,0:T(8,128)(2,1)}, bf16[384,768]{1,0:T(8,128)(2,1)}, u32[]{:S(2)}, u32[]{:S(2)}) collective-permute-start(bf16[384,768]{1,0:T(8,128)(2,1)} %get-tuple-element.231), channel_id=1, source_target_pairs={{0,2},{1,3},{2,0},{3,1},{4,6},{5,7},{6,4},{7,5},{8,10},{9,11},{10,... | collective-permute-start | bytes 1769480 | tf_op jit(solution)/shard_map/ppermute | solution.py:724
  212.9 21.2 %collective-permute-start.42 = (bf16[96,768]{1,0:T(8,128)(2,1)}, bf16[96,768]{1,0:T(8,128)(2,1)}, u32[]{:S(2)}, u32[]{:S(2)}) collective-permute-start(bf16[96,768]{1,0:T(8,128)(2,1)} %get-tuple-element.342), channel_id=1, source_target_pairs={{0,16},{4,20},{8,24},{12,28},{16,0},{20,4},{24,8},{28,12},{1,17},{... | collective-permute-start | bytes 442376 | tf_op jit(solution)/shard_map/ppermute | solution.py:765
  217.2 16.9 %collective-permute-start.43 = (bf16[96,768]{1,0:T(8,128)(2,1)}, bf16[96,768]{1,0:T(8,128)(2,1)}, u32[]{:S(2)}, u32[]{:S(2)}) collective-permute-start(bf16[96,768]{1,0:T(8,128)(2,1)} %get-tuple-element.340), channel_id=1, source_target_pairs={{0,16},{4,20},{8,24},{12,28},{16,0},{20,4},{24,8},{28,12},{1,17},{... | collective-permute-start | bytes 442376 | tf_op jit(solution)/shard_map/ppermute | solution.py:765
  239.0 14.0 %collective-permute-start.45 = (bf16[4,64,512]{2,1,0:T(8,128)(2,1)S(1)}, bf16[4,64,512]{2,1,0:T(8,128)(2,1)S(1)}, u32[]{:S(2)}, u32[]{:S(2)}) collective-permute-start(bf16[4,64,512]{2,1,0:T(8,128)(2,1)S(1)} %add_convert_fusion.13.l0), channel_id=1, source_target_pairs={{0,2},{1,3},{2,0},{3,1},{4,6},{5,7},{6,4},{7,5},{8,10},{9,11},{10,... | collective-permute-start | bytes 786440 | tf_op jit(solution)/shard_map/ppermute | solution.py:724
  253.5 15.3 %collective-permute-start.46 = (bf16[384,768]{1,0:T(8,128)(2,1)S(1)}, bf16[384,768]{1,0:T(8,128)(2,1)S(1)}, u32[]{:S(2)}, u32[]{:S(2)}) collective-permute-start(bf16[384,768]{1,0:T(8,128)(2,1)S(1)} %copy-done.68), channel_id=1, source_target_pairs={{0,2},{1,3},{2,0},{3,1},{4,6},{5,7},{6,4},{7,5},{8,10},{9,11},{10,... | collective-permute-start | bytes 1769480 | tf_op jit(solution)/shard_map/ppermute | solution.py:724
  306.7 15.7 %collective-permute-start.71 = (bf16[192,768]{1,0:T(8,128)(2,1)S(1)}, bf16[192,768]{1,0:T(8,128)(2,1)S(1)}, u32[]{:S(2)}, u32[]{:S(2)}) collective-permute-start(bf16[192,768]{1,0:T(8,128)(2,1)S(1)} %slice.235), channel_id=1, source_target_pairs={{0,4},{4,0},{8,12},{12,8},{16,20},{20,16},{24,28},{28,24},{1,5},{5... | collective-permute-start | bytes 884744 | tf_op jit(solution)/shard_map/ppermute | solution.py:765
  307.4 14.8 %collective-permute-start.70 = (bf16[192,768]{1,0:T(8,128)(2,1)S(1)}, bf16[192,768]{1,0:T(8,128)(2,1)S(1)}, u32[]{:S(2)}, u32[]{:S(2)}) collective-permute-start(bf16[192,768]{1,0:T(8,128)(2,1)S(1)} %slice.233), channel_id=1, source_target_pairs={{0,8},{4,12},{8,0},{12,4},{16,24},{20,28},{24,16},{28,20},{1,9},{5... | collective-permute-start | bytes 884744 | tf_op jit(solution)/shard_map/ppermute | solution.py:765
  (139 other events, 1254.3 us)

commit v2 on v1

--- a/solution.py
+++ b/solution.py
@@ -16,7 +16,7 @@
 HALO = TAPS // 2
 EARLY = 1
 LATE = 2
-IDLE = 1
+IDLE = 0
 GROUP = 256
 NN = ((1,), (0,))
 NT = ((1,), (1,))

time: 331 us -> 335 us (1.012)
  waiting for transfers between devices: 105 us -> 110 us
    ppermute x34, waiting for transfers between devices: 65 us -> 70 us  [hop_batch(): return lax.ppermute(x, 'batch', [(i, i ^ step) for i in range(batch_count)])]
  transfers between devices with their start and end apart: 72 -> 72, of which waited for: 34 -> 34; matrix products, arithmetic and copies ran while one was open for 8% -> 7% of each run, Pallas kernels for 30% -> 29%
where the time goes in v2:
time: 335 us; the launch traced here: 334 us
  waiting for transfers between devices  110 us (33%)
  Pallas kernels  108 us (32%)
  starting transfers between devices  64.2 us (19%)
  local copies, waits for them, and re-layouts  32 us (10%)
  other arithmetic  14.1 us (4%)
    pallas_call x14, Pallas kernels, call(): pl.pallas_call(body, out_shape=[jax.ShapeDtypeStruct(s, d) for s, d in ou...  103 us
    ppermute x34, waiting for transfers between devices, hop_batch(): return lax.ppermute(x, 'batch', [(i, i ^ step) for i in range(batch_count)])  70 us
    ppermute x36, waiting for transfers between devices, hop(): return lax.ppermute(x, 'head', [(i, i ^ HOP[step]) for i in range(4)])  40.3 us
    ppermute x34, starting transfers between devices, hop_batch(): return lax.ppermute(x, 'batch', [(i, i ^ step) for i in range(batch_count)])  39.1 us
    ppermute x36, starting transfers between devices, hop(): return lax.ppermute(x, 'head', [(i, i ^ HOP[step]) for i in range(4)])  23.7 us
    unnamed x188, local copies, waits for them, and re-layouts  21.3 us
    convert_element_type x18, other arithmetic, add_all(): (a.astype(f32) + b.astype(f32)).astype(bf16)  6.98 us
  transfers between devices with their start and end apart: 72, of which 34 were waited for; matrix products, arithmetic and copies ran while one was open for 7% of the time, Pallas kernels for 29%

profile of v2, /device:TPU:0, one launch (start us, length us, event | category | flops | bytes accessed | tf_op | source)
XLA Modules:
  0.0 333.9 jit_solution(3102256079426682421)
XLA Ops:
  14.8 8.7 %landmarks.1 = (f32[64,768]{1,0:T(8,128)S(1)}, bf16[64,768]{1,0:T(8,128)(2,1)S(1)}, f32[6,4,3,64,64]{4,3,2,1,0:T(8,128)S(1)}) custom-call(bf16[64,768]{1,0:T(8,128)(2,1)S(1)} %fusion.1.p0, bf16[64,768]{1,0:T(8,128)(2,1)S(1)} %collective-permute-done.p1, bf16[64,768]{1,0:T(8,128)(2,1)S(1)} %collective-permute-done.1.p2, ...), custom_call_target="tpu_custom_call" | custom-call | flops 1000000000 | bytes 4194304 | tf_op jit(solution)/shard_map/landmarks/pallas_call | solution.py:57
  30.1 4.5 %collective-permute-done.6 = f32[64,768]{1,0:T(8,128)S(1)} collective-permute-done((f32[64,768]{1,0:T(8,128)S(1)}, f32[64,768]{1,0:T(8,128)S(1)}, u32[]{:S(2)}, u32[]{:S(2)}) %collective-permute-start.6) | collective-permute-done | bytes 196640 | tf_op jit(solution)/shard_map/ppermute | solution.py:724
  40.7 5.4 %project.1 = (bf16[4,512,256]{2,1,0:T(8,128)(2,1)S(1)}, bf16[4,512,256]{2,1,0:T(8,128)(2,1)S(1)}, bf16[4,640,256]{2,1,0:T(8,128)(2,1)S(1)}) custom-call(s32[3]{0:T(128)S(1)} %pad_add_fusion.info.refs_7_, bf16[512,768]{1,0:T(8,128)(2,1)S(1)} %bitcast.68, bf16[32,768]{1,0:T(8,128)(2,1)S(1)} %get-tuple-element.306.before, ...), custom_call_target="tpu_custom_call" | custom-call | flops 2415919104 | bytes 8388608 | tf_op jit(solution)/shard_map/project/pallas_call | solution.py:57
  46.4 5.9 %collective-permute-done.16.o1.w1.refs_13_ = bf16[960,384]{1,0:T(8,128)(2,1)S(1)} collective-permute-done((bf16[960,384]{1,0:T(8,128)(2,1)S(1)}, bf16[960,384]{1,0:T(8,128)(2,1)S(1)}, u32[]{:S(2)}, u32[]{:S(2)}) %collective-permute-start.16) | collective-permute-done | bytes 737312 | tf_op jit(solution)/shard_map/ppermute | solution.py:724
  52.6 4.2 %third.1.p0 = bf16[4,64,256]{2,1,0:T(8,128)(2,1)S(1)} custom-call(s32[3]{0:T(128)S(1)} %pad_add_fusion.info.refs_7_, f32[4,64,768]{2,1,0:T(8,128)S(1)} %pad_maximum_fusion.lm, bf16[4,512,256]{2,1,0:T(8,128)(2,1)S(1)} %get-tuple-element.153.k_ref, bf16[4,640,256]{2,1,0:T(8,128)(2,1)S(1)} %get-tuple-element.154.v_ref), custom_call_target="tpu_custom_call" | custom-call | flops 1000000000 | bytes 3145728 | tf_op jit(solution)/shard_map/third/pallas_call | solution.py:57
  59.1 3.6 %collective-permute-done.15.p3 = bf16[4,64,256]{2,1,0:T(8,128)(2,1)S(1)} collective-permute-done((bf16[4,64,256]{2,1,0:T(8,128)(2,1)S(1)}, bf16[4,64,256]{2,1,0:T(8,128)(2,1)S(1)}, u32[]{:S(2)}, u32[]{:S(2)}) %collective-permute-start.15) | collective-permute-done | bytes 131104 | tf_op jit(solution)/shard_map/ppermute | solution.py:724
  64.9 6.7 %context.1 = (bf16[4,512,256]{2,1,0:T(8,128)(2,1)S(1)}, f32[4,64,256]{2,1,0:T(8,128)S(1)}, f32[4,64,256]{2,1,0:T(8,128)S(1)}) custom-call(bf16[4,64,256]{2,1,0:T(8,128)(2,1)S(1)} %third.1.p0, bf16[4,64,256]{2,1,0:T(8,128)(2,1)S(1)} %collective-permute-done.13.p1, bf16[4,64,256]{2,1,0:T(8,128)(2,1)S(1)} %collective-permute-done.14.p2, ...), custom_call_target="tpu_custom_call" | custom-call | flops 3000000000 | bytes 5242880 | tf_op jit(solution)/shard_map/context/pallas_call | solution.py:57
  73.0 4.9 %collective-permute-done.21.w1 = bf16[768,384]{1,0:T(8,128)(2,1)S(1)} collective-permute-done((bf16[768,384]{1,0:T(8,128)(2,1)S(1)}, bf16[768,384]{1,0:T(8,128)(2,1)S(1)}, u32[]{:S(2)}, u32[]{:S(2)}) %collective-permute-start.21) | collective-permute-done | bytes 589856 | tf_op jit(solution)/shard_map/ppermute | solution.py:724
  83.0 9.0 %collective-permute-done.22.w2 = bf16[768,384]{1,0:T(8,128)(2,1)S(1)} collective-permute-done((bf16[768,384]{1,0:T(8,128)(2,1)S(1)}, bf16[768,384]{1,0:T(8,128)(2,1)S(1)}, u32[]{:S(2)}, u32[]{:S(2)}) %collective-permute-start.22) | collective-permute-done | bytes 589856 | tf_op jit(solution)/shard_map/ppermute | solution.py:765
  92.7 8.7 %up.1 = (bf16[4,512,768]{2,1,0:T(8,128)(2,1)S(1)}, bf16[4,512,768]{2,1,0:T(8,128)(2,1)}, bf16[3,512,768]{2,1,0:T(8,128)(2,1)}) custom-call(s32[3]{0:T(128)S(1)} %pad_add_fusion.info.refs_7_, bf16[512,768]{1,0:T(8,128)(2,1)S(1)} %get-tuple-element.163.low.refs_6_, f32[4,8,768]{2,1,0:T(8,128)S(1)} %pad_maximum_fusion.11.small, ...), custom_call_target="tpu_custom_call" | custom-call | flops 2415919104 | bytes 12582912 | tf_op jit(solution)/shard_map/up/pallas_call | solution.py:57
  101.6 6.5 %down.1 = (bf16[512,768]{1,0:T(8,128)(2,1)}, f32[512,768]{1,0:T(8,128)S(1)}, bf16[512,768]{1,0:T(8,128)(2,1)S(1)}, f32[8,768]{1,0:T(8,128)S(1)}) custom-call(s32[3]{0:T(128)S(1)} %pad_add_fusion.info.refs_7_, bf16[4,512,768]{2,1,0:T(8,128)(2,1)S(1)} %get-tuple-element.164.hidden.refs_1_, f32[512,768]{1,0:T(8,128)S(1)} %get-tuple-element.165.normed, ...), custom_call_target="tpu_custom_call" | custom-call | flops 2415919104 | bytes 14680064 | tf_op jit(solution)/shard_map/down/pallas_call | solution.py:57
  109.2 6.4 %hidden_back.1 = (bf16[4,512,768]{2,1,0:T(8,128)(2,1)S(1)}, bf16[3,512,768]{2,1,0:T(8,128)(2,1)}, f32[4,8,768]{2,1,0:T(8,128)S(1)}) custom-call(s32[3]{0:T(128)S(1)} %pad_add_fusion.info.refs_7_, bf16[512,768]{1,0:T(8,128)(2,1)S(1)} %get-tuple-element.178.dlow.refs_3_, bf16[4,512,768]{2,1,0:T(8,128)(2,1)S(1)} %copy-done.73, bf16[768,768]{1,0:T(8,128)(2,1)S(1)} %copy-done.30, ...), custom_call_target="tpu_custom_call" | custom-call | flops 2415919104 | bytes 12582912 | tf_op jit(solution)/shard_map/hidden_back/pallas_call | solution.py:57
  118.5 4.4 %collective-permute-done.27.refs_4_ = bf16[3,512,768]{2,1,0:T(8,128)(2,1)} collective-permute-done((bf16[3,512,768]{2,1,0:T(8,128)(2,1)}, bf16[3,512,768]{2,1,0:T(8,128)(2,1)}, u32[]{:S(2)}, u32[]{:S(2)}) %collective-permute-start.27) | collective-permute-done | bytes 2359328 | tf_op jit(solution)/shard_map/ppermute | solution.py:724
  125.2 7.1 %grad_sent.1 = (bf16[384,768]{1,0:T(8,128)(2,1)}, bf16[384,768]{1,0:T(8,128)(2,1)S(1)}, bf16[384,768]{1,0:T(8,128)(2,1)}, bf16[384,768]{1,0:T(8,128)(2,1)S(1)}) custom-call(s32[2]{0:T(128)S(1)} %get-tuple-element.287.refs_0_, bf16[4,512,768]{2,1,0:T(8,128)(2,1)} %copy-done.1, bf16[3,512,768]{2,1,0:T(8,128)(2,1)} %collective-permute-done.26.refs_2_, ...), custom_call_target="tpu_custom_call" | custom-call | flops 5000000000 | bytes 10485760 | tf_op jit(solution)/shard_map/grad_sent/pallas_call | solution.py:57
  136.1 15.2 %grad_kept.1 = (bf16[384,768]{1,0:T(8,128)(2,1)S(1)}, bf16[384,768]{1,0:T(8,128)(2,1)S(1)}, bf16[384,768]{1,0:T(8,128)(2,1)S(1)}, bf16[384,768]{1,0:T(8,128)(2,1...) custom-call(s32[2]{0:T(128)S(1)} %get-tuple-element.288.refs_0_, ...), custom_call_target="tpu_custom_call" | custom-call | flops 5000000000 | bytes 10485760 | tf_op jit(solution)/shard_map/grad_kept/pallas_call | solution.py:57
  157.6 9.4 %first_back.1 = (f32[4,64,256]{2,1,0:T(8,128)S(1)}, bf16[4,512,256]{2,1,0:T(8,128)(2,1)S(1)}, f32[4,64,256]{2,1,0:T(8,128)S(1)}, f32[4,512,256]{2,1,0:T(8,128)S(1)}, f32[4,8,256]{2,1,0:T(8,128)S(1)}) custom-call(s32[3]{0:T(128)S(1)} %pad_add_fusion.info.refs_7_, bf16[512,768]{1,0:T(8,128)(2,1)S(1)} %get-tuple-element.242.g_ref.g, ...), custom_call_target="tpu_custom_call" | custom-call | flops 5000000000 | bytes 10485760 | tf_op jit(solution)/shard_map/first_back/pallas_call | solution.py:57
  174.1 11.3 %collective-permute-done.36 = bf16[2,192,768]{2,1,0:T(8,128)(2,1)S(1)} collective-permute-done((bf16[2,192,768]{2,1,0:T(8,128)(2,1)S(1)}, bf16[2,192,768]{2,1,0:T(8,128)(2,1)S(1)}, u32[]{:S(2)}, u32[]{:S(2)}) %collective-permute-start.36) | collective-permute-done | bytes 589856 | tf_op jit(solution)/shard_map/ppermute | solution.py:765
  189.6 4.9 %third_back.1 = (bf16[4,512,768]{2,1,0:T(8,128)(2,1)S(1)}, bf16[2,512,1024]{2,1,0:T(8,128)(2,1)S(1)}, f32[4,64,512]{2,1,0:T(8,128)S(1)}) custom-call(s32[3]{0:T(128)S(1)} %pad_add_fusion.info.refs_7_, f32[4,64,256]{2,1,0:T(8,128)S(1)} %maximum_add_fusion.1.x0, f32[4,64,256]{2,1,0:T(8,128)S(1)} %collective-permute-done.35.x1, f32[4,64,768]{2,1,0:T(8,128)S(1)} %copy-done.44, ...), custom_call_target="tpu_custom_call" | custom-call | flops 5000000000 | bytes 8388608 | tf_op jit(solution)/shard_map/third_back/pallas_call | solution.py:57
  197.4 4.2 %collective-permute-done.38 = bf16[192,768]{1,0:T(8,128)(2,1)S(1)} collective-permute-done((bf16[192,768]{1,0:T(8,128)(2,1)S(1)}, bf16[192,768]{1,0:T(8,128)(2,1)S(1)}, u32[]{:S(2)}, u32[]{:S(2)}) %collective-permute-start.38) | collective-permute-done | bytes 294944 | tf_op jit(solution)/shard_map/ppermute | solution.py:724
  224.7 9.4 %inverse_back.1 = bf16[4,64,512]{2,1,0:T(8,128)(2,1)S(1)} custom-call(f32[4,64,256]{2,1,0:T(8,128)S(1)} %maximum_add_fusion.1.x0, f32[4,64,256]{2,1,0:T(8,128)S(1)} %copy-done.60, f32[4,64,256]{2,1,0:T(8,128)S(1)} %copy-done.58, f32[64,768]{1,0:T(8,128)S(1)} %copy-done.42, f32[6,4,3,64,64]{4,3,2,1,0:T(8,128)S(1)} %copy-done.32, f32[4,64,512]{2,1,0:T(8,128)S(1)} %copy-done.47), custom_call_target="tpu_custom_call" | custom-call | flops 1000000000 | bytes 4194304 | tf_op jit(solution)/shard_map/inverse_back/pallas_call | solution.py:57
  239.7 10.2 %collective-permute-done.51 = bf16[96,768]{1,0:T(8,128)(2,1)S(1)} collective-permute-done((bf16[96,768]{1,0:T(8,128)(2,1)S(1)}, bf16[96,768]{1,0:T(8,128)(2,1)S(1)}, u32[]{:S(2)}, u32[]{:S(2)}) %collective-permute-start.51) | collective-permute-done | bytes 147488 | tf_op jit(solution)/shard_map/ppermute | solution.py:765
  254.9 7.4 %token_back.1 = f32[512,768]{1,0:T(8,128)} custom-call(s32[3]{0:T(128)S(1)} %pad_add_fusion.info.refs_7_, bf16[4,64,512]{2,1,0:T(8,128)(2,1)S(1)} %add_convert_fusion.13.l0, bf16[4,64,512]{2,1,0:T(8,128)(2,1)S(1)} %collective-permute-done.45.l1, bf16[4,512,768]{2,1,0:T(8,128)(2,1)S(1)} %get-tuple-element.237.joint, f32[512,768]{1,0:T(8,128)S(1)} %copy-done.35, ...), custom_call_target="tpu_custom_call" | custom-call | flops 2415919104 | bytes 10485760 | tf_op jit(solution)/shard_map/token_back/pallas_call | solution.py:57
  274.0 4.9 %collective-permute-done.48 = bf16[192,768]{1,0:T(8,128)(2,1)S(1)} collective-permute-done((bf16[192,768]{1,0:T(8,128)(2,1)S(1)}, bf16[192,768]{1,0:T(8,128)(2,1)S(1)}, u32[]{:S(2)}, u32[]{:S(2)}) %collective-permute-start.48) | collective-permute-done | bytes 294944 | tf_op jit(solution)/shard_map/ppermute | solution.py:765
  290.0 5.1 %collective-permute-done.53 = bf16[192,768]{1,0:T(8,128)(2,1)S(1)} collective-permute-done((bf16[192,768]{1,0:T(8,128)(2,1)S(1)}, bf16[192,768]{1,0:T(8,128)(2,1)S(1)}, u32[]{:S(2)}, u32[]{:S(2)}) %collective-permute-start.53) | collective-permute-done | bytes 294944 | tf_op jit(solution)/shard_map/ppermute | solution.py:765
  (449 shorter events, 162.7 us)
Async XLA Ops:
  6.1 21.6 %collective-permute-start.5 = (bf16[512,768]{1,0:T(8,128)(2,1)S(1)}, bf16[512,768]{1,0:T(8,128)(2,1)S(1)}, u32[]{:S(2)}, u32[]{:S(2)}) collective-permute-start(bf16[512,768]{1,0:T(8,128)(2,1)S(1)} %bitcast.67), channel_id=1, source_target_pairs={{0,1},{1,0},{2,3},{3,2},{4,5},{5,4},{6,7},{7,6},{8,9},{9,8},{10,11... | collective-permute-start | bytes 2359304 | tf_op jit(solution)/shard_map/ppermute | solution.py:724
  8.7 27.0 %collective-permute-start.10 = (bf16[608,768]{1,0:T(8,128)(2,1)S(1)}, bf16[608,768]{1,0:T(8,128)(2,1)}, u32[]{:S(2)}, u32[]{:S(2)}) collective-permute-start(bf16[608,768]{1,0:T(8,128)(2,1)S(1)} %constant_dynamic-update-slice_fusion.wt.w0), channel_id=1, source_target_pairs={{0,1},{1,0},{2,3},{3,2},{4,5},{5,4},{6,7},{7,6},{8,9},{9,8},{10,11... | collective-permute-start | bytes 2801672 | tf_op jit(solution)/shard_map/ppermute | solution.py:724
  10.5 17.2 %collective-permute-start.4 = (bf16[32,768]{1,0:T(8,128)(2,1)S(1)}, bf16[32,768]{1,0:T(8,128)(2,1)S(1)}, u32[]{:S(2)}, u32[]{:S(2)}) collective-permute-start(bf16[32,768]{1,0:T(8,128)(2,1)S(1)} %select_bitcast_fusion), channel_id=1, source_target_pairs={{1,2},{2,1},{5,6},{6,5},{9,10},{10,9},{13,14},{14,13},{17,18},{18,... | collective-permute-start | bytes 147464 | tf_op jit(solution)/shard_map/ppermute | solution.py:769
  11.2 14.5 %collective-permute-start.3 = (bf16[608,384]{1,0:T(8,128)(2,1)S(1)}, bf16[608,384]{1,0:T(8,128)(2,1)S(1)}, u32[]{:S(2)}, u32[]{:S(2)}) collective-permute-start(bf16[608,384]{1,0:T(8,128)(2,1)S(1)} %constant_dynamic-slice_fusion.16), channel_id=1, source_target_pairs={{0,2},{1,3},{2,0},{3,1},{4,6},{5,7},{6,4},{7,5},{8,10},{9,11},{10,... | collective-permute-start | bytes 1400840 | tf_op jit(solution)/shard_map/ppermute | solution.py:724
  34.6 17.6 %collective-permute-start.16 = (bf16[960,384]{1,0:T(8,128)(2,1)S(1)}, bf16[960,384]{1,0:T(8,128)(2,1)S(1)}, u32[]{:S(2)}, u32[]{:S(2)}) collective-permute-start(bf16[960,384]{1,0:T(8,128)(2,1)S(1)} %constant_dynamic-slice_fusion.15), channel_id=1, source_target_pairs={{0,2},{1,3},{2,0},{3,1},{4,6},{5,7},{6,4},{7,5},{8,10},{9,11},{10,... | collective-permute-start | bytes 2211848 | tf_op jit(solution)/shard_map/ppermute | solution.py:724
  46.2 32.7 %collective-permute-start.18 = (bf16[960,768]{1,0:T(8,128)(2,1)S(1)}, bf16[960,768]{1,0:T(8,128)(2,1)S(1)}, u32[]{:S(2)}, u32[]{:S(2)}) collective-permute-start(bf16[960,768]{1,0:T(8,128)(2,1)S(1)} %constant_dynamic-update-slice_fusion.4), channel_id=1, source_target_pairs={{0,1},{1,0},{2,3},{3,2},{4,5},{5,4},{6,7},{7,6},{8,9},{9,8},{10,11... | collective-permute-start | bytes 4423688 | tf_op jit(solution)/shard_map/ppermute | solution.py:724
  52.3 20.1 %collective-permute-start.17 = (bf16[960,384]{1,0:T(8,128)(2,1)S(1)}, bf16[960,384]{1,0:T(8,128)(2,1)S(1)}, u32[]{:S(2)}, u32[]{:S(2)}) collective-permute-start(bf16[960,384]{1,0:T(8,128)(2,1)S(1)} %collective-permute-done.16.o1.w1.refs_13_), channel_id=1, source_target_pairs={{0,4},{4,0},{8,12},{12,8},{16,20},{20,16},{24,28},{28,24},{1,5},{5... | collective-permute-start | bytes 2211848 | tf_op jit(solution)/shard_map/ppermute | solution.py:765
  62.7 15.1 %collective-permute-start.21 = (bf16[768,384]{1,0:T(8,128)(2,1)S(1)}, bf16[768,384]{1,0:T(8,128)(2,1)S(1)}, u32[]{:S(2)}, u32[]{:S(2)}) collective-permute-start(bf16[768,384]{1,0:T(8,128)(2,1)S(1)} %constant_dynamic-slice_fusion.14), channel_id=1, source_target_pairs={{0,2},{1,3},{2,0},{3,1},{4,6},{5,7},{6,4},{7,5},{8,10},{9,11},{10,... | collective-permute-start | bytes 1769480 | tf_op jit(solution)/shard_map/ppermute | solution.py:724
  77.9 14.2 %collective-permute-start.22 = (bf16[768,384]{1,0:T(8,128)(2,1)S(1)}, bf16[768,384]{1,0:T(8,128)(2,1)S(1)}, u32[]{:S(2)}, u32[]{:S(2)}) collective-permute-start(bf16[768,384]{1,0:T(8,128)(2,1)S(1)} %collective-permute-done.21.w1), channel_id=1, source_target_pairs={{0,4},{4,0},{8,12},{12,8},{16,20},{20,16},{24,28},{28,24},{1,5},{5... | collective-permute-start | bytes 1769480 | tf_op jit(solution)/shard_map/ppermute | solution.py:765
  78.8 22.7 %collective-permute-start.23 = (bf16[768,768]{1,0:T(8,128)(2,1)S(1)}, bf16[768,768]{1,0:T(8,128)(2,1)S(1)}, u32[]{:S(2)}, u32[]{:S(2)}) collective-permute-start(bf16[768,768]{1,0:T(8,128)(2,1)S(1)} %copy-done.30), channel_id=1, source_target_pairs={{0,1},{1,0},{2,3},{3,2},{4,5},{5,4},{6,7},{7,6},{8,9},{9,8},{10,11... | collective-permute-start | bytes 3538952 | tf_op jit(solution)/shard_map/ppermute | solution.py:724
  101.4 17.1 %collective-permute-start.26 = (bf16[3,512,768]{2,1,0:T(8,128)(2,1)}, bf16[3,512,768]{2,1,0:T(8,128)(2,1)}, u32[]{:S(2)}, u32[]{:S(2)}) collective-permute-start(bf16[3,512,768]{2,1,0:T(8,128)(2,1)} %get-tuple-element.172), channel_id=1, source_target_pairs={{0,1},{1,0},{2,3},{3,2},{4,5},{5,4},{6,7},{7,6},{8,9},{9,8},{10,11... | collective-permute-start | bytes 7077896 | tf_op jit(solution)/shard_map/ppermute | solution.py:724
  133.9 17.4 %collective-permute-start.29 = (bf16[384,768]{1,0:T(8,128)(2,1)}, bf16[384,768]{1,0:T(8,128)(2,1)}, u32[]{:S(2)}, u32[]{:S(2)}) collective-permute-start(bf16[384,768]{1,0:T(8,128)(2,1)} %get-tuple-element.182), channel_id=1, source_target_pairs={{0,8},{4,12},{8,0},{12,4},{16,24},{20,28},{24,16},{28,20},{1,9},{5... | collective-permute-start | bytes 1769480 | tf_op jit(solution)/shard_map/ppermute | solution.py:765
  134.6 16.7 %collective-permute-start.28 = (bf16[384,768]{1,0:T(8,128)(2,1)}, bf16[384,768]{1,0:T(8,128)(2,1)}, u32[]{:S(2)}, u32[]{:S(2)}) collective-permute-start(bf16[384,768]{1,0:T(8,128)(2,1)} %get-tuple-element.177), channel_id=1, source_target_pairs={{0,4},{4,0},{8,12},{12,8},{16,20},{20,16},{24,28},{28,24},{1,5},{5... | collective-permute-start | bytes 1769480 | tf_op jit(solution)/shard_map/ppermute | solution.py:765
  152.1 14.8 %collective-permute-start.33 = (bf16[384,768]{1,0:T(8,128)(2,1)S(1)}, bf16[384,768]{1,0:T(8,128)(2,1)S(1)}, u32[]{:S(2)}, u32[]{:S(2)}) collective-permute-start(bf16[384,768]{1,0:T(8,128)(2,1)S(1)} %copy-done.72), channel_id=1, source_target_pairs={{0,8},{4,12},{8,0},{12,4},{16,24},{20,28},{24,16},{28,20},{1,9},{5... | collective-permute-start | bytes 1769480 | tf_op jit(solution)/shard_map/ppermute | solution.py:765
  152.6 14.4 %collective-permute-start.32 = (bf16[384,768]{1,0:T(8,128)(2,1)S(1)}, bf16[384,768]{1,0:T(8,128)(2,1)S(1)}, u32[]{:S(2)}, u32[]{:S(2)}) collective-permute-start(bf16[384,768]{1,0:T(8,128)(2,1)S(1)} %copy-done.70), channel_id=1, source_target_pairs={{0,4},{4,0},{8,12},{12,8},{16,20},{20,16},{24,28},{28,24},{1,5},{5... | collective-permute-start | bytes 1769480 | tf_op jit(solution)/shard_map/ppermute | solution.py:765
  170.2 15.3 %collective-permute-start.36 = (bf16[2,192,768]{2,1,0:T(8,128)(2,1)S(1)}, bf16[2,192,768]{2,1,0:T(8,128)(2,1)S(1)}, u32[]{:S(2)}, u32[]{:S(2)}) collective-permute-start(bf16[2,192,768]{2,1,0:T(8,128)(2,1)S(1)} %pad_maximum_fusion.1), channel_id=1, source_target_pairs={{0,8},{4,12},{8,0},{12,4},{16,24},{20,28},{24,16},{28,20},{1,9},{5... | collective-permute-start | bytes 1769480 | tf_op jit(solution)/shard_map/ppermute | solution.py:765
  172.0 15.0 %collective-permute-start.37 = (bf16[2,192,768]{2,1,0:T(8,128)(2,1)S(1)}, bf16[2,192,768]{2,1,0:T(8,128)(2,1)S(1)}, u32[]{:S(2)}, u32[]{:S(2)}) collective-permute-start(bf16[2,192,768]{2,1,0:T(8,128)(2,1)S(1)} %pad_maximum_fusion.2), channel_id=1, source_target_pairs={{0,4},{4,0},{8,12},{12,8},{16,20},{20,16},{24,28},{28,24},{1,5},{5... | collective-permute-start | bytes 1769480 | tf_op jit(solution)/shard_map/ppermute | solution.py:765
  209.4 24.7 %collective-permute-start.41 = (bf16[384,768]{1,0:T(8,128)(2,1)}, bf16[384,768]{1,0:T(8,128)(2,1)}, u32[]{:S(2)}, u32[]{:S(2)}) collective-permute-start(bf16[384,768]{1,0:T(8,128)(2,1)} %get-tuple-element.229), channel_id=1, source_target_pairs={{0,2},{1,3},{2,0},{3,1},{4,6},{5,7},{6,4},{7,5},{8,10},{9,11},{10,... | collective-permute-start | bytes 1769480 | tf_op jit(solution)/shard_map/ppermute | solution.py:724
  212.9 21.2 %collective-permute-start.42 = (bf16[96,768]{1,0:T(8,128)(2,1)}, bf16[96,768]{1,0:T(8,128)(2,1)}, u32[]{:S(2)}, u32[]{:S(2)}) collective-permute-start(bf16[96,768]{1,0:T(8,128)(2,1)} %get-tuple-element.338), channel_id=1, source_target_pairs={{0,16},{4,20},{8,24},{12,28},{16,0},{20,4},{24,8},{28,12},{1,17},{... | collective-permute-start | bytes 442376 | tf_op jit(solution)/shard_map/ppermute | solution.py:765
  217.2 16.9 %collective-permute-start.43 = (bf16[96,768]{1,0:T(8,128)(2,1)}, bf16[96,768]{1,0:T(8,128)(2,1)}, u32[]{:S(2)}, u32[]{:S(2)}) collective-permute-start(bf16[96,768]{1,0:T(8,128)(2,1)} %get-tuple-element.336), channel_id=1, source_target_pairs={{0,16},{4,20},{8,24},{12,28},{16,0},{20,4},{24,8},{28,12},{1,17},{... | collective-permute-start | bytes 442376 | tf_op jit(solution)/shard_map/ppermute | solution.py:765
  239.0 14.0 %collective-permute-start.45 = (bf16[4,64,512]{2,1,0:T(8,128)(2,1)S(1)}, bf16[4,64,512]{2,1,0:T(8,128)(2,1)S(1)}, u32[]{:S(2)}, u32[]{:S(2)}) collective-permute-start(bf16[4,64,512]{2,1,0:T(8,128)(2,1)S(1)} %add_convert_fusion.13.l0), channel_id=1, source_target_pairs={{0,2},{1,3},{2,0},{3,1},{4,6},{5,7},{6,4},{7,5},{8,10},{9,11},{10,... | collective-permute-start | bytes 786440 | tf_op jit(solution)/shard_map/ppermute | solution.py:724
  253.5 15.3 %collective-permute-start.46 = (bf16[384,768]{1,0:T(8,128)(2,1)S(1)}, bf16[384,768]{1,0:T(8,128)(2,1)S(1)}, u32[]{:S(2)}, u32[]{:S(2)}) collective-permute-start(bf16[384,768]{1,0:T(8,128)(2,1)S(1)} %copy-done.68), channel_id=1, source_target_pairs={{0,2},{1,3},{2,0},{3,1},{4,6},{5,7},{6,4},{7,5},{8,10},{9,11},{10,... | collective-permute-start | bytes 1769480 | tf_op jit(solution)/shard_map/ppermute | solution.py:724
  299.5 25.3 %collective-permute-start.71 = (bf16[192,768]{1,0:T(8,128)(2,1)S(1)}, bf16[192,768]{1,0:T(8,128)(2,1)S(1)}, u32[]{:S(2)}, u32[]{:S(2)}) collective-permute-start(bf16[192,768]{1,0:T(8,128)(2,1)S(1)} %slice.235), channel_id=1, source_target_pairs={{0,4},{4,0},{8,12},{12,8},{16,20},{20,16},{24,28},{28,24},{1,5},{5... | collective-permute-start | bytes 884744 | tf_op jit(solution)/shard_map/ppermute | solution.py:765
  300.2 24.5 %collective-permute-start.70 = (bf16[192,768]{1,0:T(8,128)(2,1)S(1)}, bf16[192,768]{1,0:T(8,128)(2,1)S(1)}, u32[]{:S(2)}, u32[]{:S(2)}) collective-permute-start(bf16[192,768]{1,0:T(8,128)(2,1)S(1)} %slice.233), channel_id=1, source_target_pairs={{0,8},{4,12},{8,0},{12,4},{16,24},{20,28},{24,16},{28,20},{1,9},{5... | collective-permute-start | bytes 884744 | tf_op jit(solution)/shard_map/ppermute | solution.py:765
  (139 other events, 1259.5 us)
